TPU v7x, 32 devices: a whole 2x2x4 slice. The times are simulated.
32 devices in a mesh: dp: 2 (over x), seq: 4 (over z), tensor: 4 (over y, core).
Axes of the slice: x: 2, y: 2, z: 4, core: 2. Of those that a mesh axis runs over, the one named last changes fastest.
Arguments:
- tokens: float32 [4, 512, 768], P('dp', 'seq'), may hold values from -8 to 8
- positions: int32 [4, 512], P('dp', 'seq'), may hold values from 0 to 509, as said below
- qkv_weight: bfloat16 [768, 3, 768], P(('dp', 'seq'), None, 'tensor'), may hold values from -2 to 2
- attn_out_weight: bfloat16 [768, 768], P('tensor', ('dp', 'seq')), may hold values from -0.75 to 0.75
- mlp_in_weight: bfloat16 [768, 2, 1152], P(('dp', 'seq'), None, 'tensor'), may hold values from -0.21875 to 0.21875
- mlp_out_weight: bfloat16 [1152, 768], P('tensor', ('dp', 'seq')), may hold values from -0.1875 to 0.1875
- attn_gain: bfloat16 [768], P(('dp', 'seq')), may hold values from 0.25 to 1.75
- mlp_gain: bfloat16 [768], P(('dp', 'seq')), may hold values from 0.25 to 1.75
- cotangent: float32 [4, 512, 768], P('dp', 'seq'), may hold values from -6 to 6
Outputs:
- output: float32 [4, 512, 768], P('dp', 'seq')
- grad_tokens: float32 [4, 512, 768], P('dp', 'seq')
- grad_qkv: float32 [768, 3, 768], P(('dp', 'seq'), None, 'tensor')
- grad_attn_out: float32 [768, 768], P('tensor', ('dp', 'seq'))
- grad_mlp_in: float32 [768, 2, 1152], P(('dp', 'seq'), None, 'tensor')
- grad_mlp_out: float32 [1152, 768], P('tensor', ('dp', 'seq'))
- grad_attn_gain: float32 [768], P(('dp', 'seq'))
- grad_mlp_gain: float32 [768], P(('dp', 'seq'))
Inputs may be any that keep to these rules, and one draw needn't show every extreme that they name: Each sequence packs three documents: the first ends within the first 64 positions, the last begins within the last 64 positions; a position counts the tokens before it in its own document.
All inputs are finite; a program needn't handle non-finite values.
Results may differ from a plain program's by a relative error of at most 0.014.
Values may be sent and summed in bfloat16 or wider, within the bound.
A program may use at most 128 MiB of HBM per device.

v0:
```python
import math

import jax
import jax.numpy as jnp
from jax import lax
from jax.sharding import PartitionSpec as P

D = 768
HD = 64


EPS = 1e-05
ROPE_BASE = 160000.0
INV_ROOT2 = 0.7071067811865476
INV_ROOT2PI = 0.3989422804014327


def apply_layer_norm(values):
    row_average = jnp.mean(values, axis=-1, keepdims=True)
    centred = values - row_average
    inverse_deviation = lax.rsqrt(jnp.mean(centred * centred, axis=-1, keepdims=True) + EPS)
    return (centred * inverse_deviation, inverse_deviation)


def norm_backward_pass(centered_gradient, standardized_input, inverse_deviation):
    first_result = jnp.mean(centered_gradient, axis=-1, keepdims=True)
    second_result = jnp.mean(centered_gradient * standardized_input, axis=-1, keepdims=True)
    return inverse_deviation * (
        centered_gradient - first_result - standardized_input * second_result
    )


def rope_tables(places, width):
    half = width // 2
    ramp = jnp.arange(half, dtype=jnp.float32) * (2.0 / width)
    freq = jnp.exp(-math.log(ROPE_BASE) * ramp)
    angle = places.astype(jnp.float32)[:, None] * freq[None, :]
    cosine = jnp.cos(angle)
    sine = jnp.sin(angle)
    return (jnp.concatenate([cosine, cosine], axis=-1), jnp.concatenate([sine, sine], axis=-1))


def rotate(values, cosine, sine):
    half = values.shape[-1] // 2
    turned = jnp.concatenate([-values[..., half:], values[..., :half]], axis=-1)
    return values * cosine[:, None, :] + turned * sine[:, None, :]


def unrotate(grads, cosine, sine):
    half = grads.shape[-1] // 2
    moved = grads * sine[:, None, :]
    back = jnp.concatenate([moved[..., half:], -moved[..., :half]], axis=-1)
    return grads * cosine[:, None, :] + back


def gelu_parts(input_rows):
    cdf = 0.5 * (1.0 + jax.scipy.special.erf(input_rows * INV_ROOT2))
    return (
        input_rows * cdf,
        cdf + input_rows * jnp.exp(-0.5 * input_rows * input_rows) * INV_ROOT2PI,
    )


def masked_scores(queries, keys, q_start, k_start):
    scale = 1.0 / math.sqrt(queries.shape[-1])
    scores = jnp.dot(queries, keys.T, preferred_element_type=jnp.float32) * scale
    return jnp.where(q_start[:, None] == k_start[None, :], scores, -jnp.inf)


def head_forward(queries, keys, values, q_start, k_start):
    scores = masked_scores(queries, keys, q_start, k_start)
    top = jnp.max(scores, axis=-1, keepdims=True)
    lse = top[:, 0] + jnp.log(jnp.sum(jnp.exp(scores - top), axis=-1))
    probs = jnp.exp(scores - lse[:, None]).astype(jnp.bfloat16)
    context = jnp.dot(probs, values, preferred_element_type=jnp.float32).astype(jnp.bfloat16)
    return (context, lse)


def score_grads(queries, keys, values, dcontext, lse, delta, q_start, k_start):
    scale = 1.0 / math.sqrt(queries.shape[-1])
    scores = masked_scores(queries, keys, q_start, k_start)
    probs = jnp.exp(scores - lse[:, None])
    dprobs = jnp.dot(dcontext, values.T, preferred_element_type=jnp.float32)
    dscores = (probs * (dprobs - delta[:, None]) * scale).astype(jnp.bfloat16)
    return (probs.astype(jnp.bfloat16), dscores)


def tensor_total(partial_sum):
    return lax.psum(partial_sum, "tensor")


def per_device(
    tokens,
    positions,
    qkv_weight,
    attn_out_weight,
    mlp_in_weight,
    mlp_out_weight,
    attn_gain,
    mlp_gain,
    cotangent,
):
    seqs_here = tokens.shape[0]
    rows = tokens.shape[1]
    local_width = qkv_weight.shape[2]
    heads_here = local_width // HD
    units_here = mlp_out_weight.shape[0]
    shards = (qkv_weight, attn_out_weight, mlp_in_weight, mlp_out_weight, attn_gain, mlp_gain)
    all_places = lax.all_gather(positions, "seq", axis=1, tiled=True)
    full_length = all_places.shape[1]
    first_row = lax.axis_index("seq") * rows
    local_index = first_row + jnp.arange(rows, dtype=jnp.int32)
    every_index = jnp.arange(full_length, dtype=jnp.int32)
    g_qkv = jnp.zeros((D, 3, local_width), jnp.float32)
    g_attn_out = jnp.zeros((local_width, D), jnp.float32)
    g_mlp_in = jnp.zeros((D, 2, units_here), jnp.float32)
    g_mlp_out = jnp.zeros((units_here, D), jnp.float32)
    attention_gain_gradient = jnp.zeros((D,), jnp.float32)
    feedforward_gain_gradient = jnp.zeros((D,), jnp.float32)
    outputs = []
    input_gradient_total = []
    for micro in range(seqs_here):
        input_rows = tokens[micro]
        output_gradient = cotangent[micro]
        local_starts = local_index - positions[micro]
        every_starts = every_index - all_places[micro]
        cosine, sine = rope_tables(positions[micro], HD)
        gathered = (
            lax.all_gather(shards[0], ("dp", "seq"), axis=0, tiled=True),
            lax.all_gather(shards[1], ("dp", "seq"), axis=1, tiled=True),
            lax.all_gather(shards[2], ("dp", "seq"), axis=0, tiled=True),
            lax.all_gather(shards[3], ("dp", "seq"), axis=1, tiled=True),
            lax.all_gather(shards[4], ("dp", "seq"), axis=0, tiled=True),
            lax.all_gather(shards[5], ("dp", "seq"), axis=0, tiled=True),
        )
        full_qkv, full_attn_out, full_in, full_out, full_gain1, full_gain2 = gathered
        attention_standardized, attention_inverse_deviation = apply_layer_norm(input_rows)
        attention_norm_gain = full_gain1.astype(jnp.float32)
        attention_normed = (attention_standardized * attention_norm_gain).astype(jnp.bfloat16)
        wide_qkv = full_qkv.reshape(D, 3 * local_width)
        qkv = jnp.dot(attention_normed, wide_qkv, preferred_element_type=jnp.float32).reshape(
            rows, 3, heads_here, HD
        )
        query = rotate(qkv[:, 0], cosine, sine).astype(jnp.bfloat16)
        key_rot = rotate(qkv[:, 1], cosine, sine).astype(jnp.bfloat16)
        value = qkv[:, 2].astype(jnp.bfloat16)
        q_heads = jnp.transpose(query, (1, 0, 2))
        k_heads = jnp.transpose(key_rot, (1, 0, 2))
        v_heads = jnp.transpose(value, (1, 0, 2))
        all_keys, all_values = (
            lax.all_gather(k_heads, "seq", axis=1, tiled=True),
            lax.all_gather(v_heads, "seq", axis=1, tiled=True),
        )
        ctx_heads, lse_heads = lax.map(
            lambda group: head_forward(group[0], group[1], group[2], local_starts, every_starts),
            (q_heads, all_keys, all_values),
        )
        context = jnp.transpose(ctx_heads, (1, 0, 2)).reshape(rows, local_width)
        middle_state = input_rows + tensor_total(
            jnp.dot(context, full_attn_out, preferred_element_type=jnp.float32)
        )
        feedforward_standardized, feedforward_inverse_deviation = apply_layer_norm(middle_state)
        feedforward_norm_gain = full_gain2.astype(jnp.float32)
        feedforward_normed = (feedforward_standardized * feedforward_norm_gain).astype(jnp.bfloat16)
        wide_in = full_in.reshape(D, 2 * units_here)
        upper = jnp.dot(feedforward_normed, wide_in, preferred_element_type=jnp.float32).reshape(
            rows, 2, units_here
        )
        active, slope = gelu_parts(upper[:, 0])
        gate = upper[:, 1]
        hidden = (active * gate).astype(jnp.bfloat16)
        outputs.append(
            middle_state
            + tensor_total(jnp.dot(hidden, full_out, preferred_element_type=jnp.float32))
        )
        regathered = (
            lax.all_gather(shards[0], ("dp", "seq"), axis=0, tiled=True),
            lax.all_gather(shards[1], ("dp", "seq"), axis=1, tiled=True),
            lax.all_gather(shards[2], ("dp", "seq"), axis=0, tiled=True),
            lax.all_gather(shards[3], ("dp", "seq"), axis=1, tiled=True),
            lax.all_gather(shards[4], ("dp", "seq"), axis=0, tiled=True),
            lax.all_gather(shards[5], ("dp", "seq"), axis=0, tiled=True),
        )
        back_qkv, back_attn_out, back_in, back_out, back_gain1, back_gain2 = regathered
        wide_qkv = back_qkv.reshape(D, 3 * local_width)
        wide_in = back_in.reshape(D, 2 * units_here)
        attention_norm_gain = back_gain1.astype(jnp.float32)
        feedforward_norm_gain = back_gain2.astype(jnp.float32)
        dyb = output_gradient.astype(jnp.bfloat16)
        g_mlp_out = g_mlp_out + jnp.dot(hidden.T, dyb, preferred_element_type=jnp.float32)
        dhidden = jnp.dot(dyb, back_out.T, preferred_element_type=jnp.float32)
        dup = (
            jnp.stack([dhidden * gate * slope, dhidden * active], axis=1)
            .astype(jnp.bfloat16)
            .reshape(rows, 2 * units_here)
        )
        g_mlp_in = g_mlp_in + jnp.dot(
            feedforward_normed.T, dup, preferred_element_type=jnp.float32
        ).reshape(D, 2, units_here)
        feedforward_normed_gradient = tensor_total(
            jnp.dot(dup, wide_in.T, preferred_element_type=jnp.float32)
        )
        feedforward_gain_gradient = feedforward_gain_gradient + jnp.sum(
            feedforward_normed_gradient * feedforward_standardized, axis=0
        )
        middle_gradient = output_gradient + norm_backward_pass(
            feedforward_normed_gradient * feedforward_norm_gain,
            feedforward_standardized,
            feedforward_inverse_deviation,
        )
        dmidb = middle_gradient.astype(jnp.bfloat16)
        g_attn_out = g_attn_out + jnp.dot(context.T, dmidb, preferred_element_type=jnp.float32)
        dcontext = jnp.dot(dmidb, back_attn_out.T, preferred_element_type=jnp.float32).astype(
            jnp.bfloat16
        )
        dc_heads = jnp.transpose(dcontext.reshape(rows, heads_here, HD), (1, 0, 2))
        delta_heads = jnp.sum(dc_heads.astype(jnp.float32) * ctx_heads.astype(jnp.float32), axis=-1)

        def back_head(group):
            qx, kx, vx, dcx, lsex, deltax = group
            probs, dscores = score_grads(qx, kx, vx, dcx, lsex, deltax, local_starts, every_starts)
            dquery = jnp.dot(dscores, kx, preferred_element_type=jnp.float32)
            dkey = jnp.dot(dscores.T, qx, preferred_element_type=jnp.float32)
            dvalue = jnp.dot(probs.T, dcx, preferred_element_type=jnp.float32)
            return (dquery, dkey, dvalue)

        dq_heads, dk_every, dv_every = lax.map(
            back_head, (q_heads, all_keys, all_values, dc_heads, lse_heads, delta_heads)
        )
        dk_heads, dv_heads = (
            lax.psum_scatter(
                dk_every.astype(jnp.bfloat16), "seq", scatter_dimension=1, tiled=True
            ).astype(jnp.float32),
            lax.psum_scatter(
                dv_every.astype(jnp.bfloat16), "seq", scatter_dimension=1, tiled=True
            ).astype(jnp.float32),
        )
        dquery = unrotate(jnp.transpose(dq_heads, (1, 0, 2)), cosine, sine)
        dkey = unrotate(jnp.transpose(dk_heads, (1, 0, 2)), cosine, sine)
        dvalue = jnp.transpose(dv_heads, (1, 0, 2))
        dqkv = (
            jnp.stack([dquery, dkey, dvalue], axis=1)
            .astype(jnp.bfloat16)
            .reshape(rows, 3 * local_width)
        )
        g_qkv = g_qkv + jnp.dot(
            attention_normed.T, dqkv, preferred_element_type=jnp.float32
        ).reshape(D, 3, local_width)
        attention_normed_gradient = tensor_total(
            jnp.dot(dqkv, wide_qkv.T, preferred_element_type=jnp.float32)
        )
        attention_gain_gradient = attention_gain_gradient + jnp.sum(
            attention_normed_gradient * attention_standardized, axis=0
        )
        input_gradient_total.append(
            middle_gradient
            + norm_backward_pass(
                attention_normed_gradient * attention_norm_gain,
                attention_standardized,
                attention_inverse_deviation,
            )
        )
    grads = (
        lax.psum_scatter(g_qkv, ("dp", "seq"), scatter_dimension=0, tiled=True),
        lax.psum_scatter(g_attn_out, ("dp", "seq"), scatter_dimension=1, tiled=True),
        lax.psum_scatter(g_mlp_in, ("dp", "seq"), scatter_dimension=0, tiled=True),
        lax.psum_scatter(g_mlp_out, ("dp", "seq"), scatter_dimension=1, tiled=True),
        lax.psum_scatter(attention_gain_gradient, ("dp", "seq"), scatter_dimension=0, tiled=True),
        lax.psum_scatter(feedforward_gain_gradient, ("dp", "seq"), scatter_dimension=0, tiled=True),
    )
    return (
        jnp.stack(outputs, axis=0),
        jnp.stack(input_gradient_total, axis=0),
        grads[0],
        grads[1],
        grads[2],
        grads[3],
        grads[4],
        grads[5],
    )


def solution(mesh):
    in_specs = (
        P("dp", "seq", None),
        P("dp", "seq"),
        P(("dp", "seq"), None, "tensor"),
        P("tensor", ("dp", "seq")),
        P(("dp", "seq"), None, "tensor"),
        P("tensor", ("dp", "seq")),
        P(("dp", "seq")),
        P(("dp", "seq")),
        P("dp", "seq", None),
    )
    out_specs = (
        P("dp", "seq", None),
        P("dp", "seq", None),
        P(("dp", "seq"), None, "tensor"),
        P("tensor", ("dp", "seq")),
        P(("dp", "seq"), None, "tensor"),
        P("tensor", ("dp", "seq")),
        P(("dp", "seq")),
        P(("dp", "seq")),
    )
    return jax.shard_map(
        per_device, mesh=mesh, in_specs=in_specs, out_specs=out_specs, check_vma=False
    )
```

profile of v0, /device:TPU:0, one launch (start us, length us, event | category | flops | bytes accessed | tf_op | source)
XLA Modules:
  0.0 749.9 jit_solution(13601899123969815073)
XLA Ops:
  13.7 23.3 %all-reduce.8 = (bf16[768]{0:T(1024)(128)(2,1)S(1)}, bf16[768]{0:T(1024)(128)(2,1)S(1)}) all-reduce(bf16[768]{0:T(1024)(128)(2,1)S(1)} %dynamic-update-slice, bf16[768]{0:T(1024)(128)(2,1)S(1)} %dynamic-update-slice.1), channel_id=1, replica_groups=mesh['dp'=2,'seq'=4,'tensor'=4] {'dp','seq'}, use_global_device_ids=true, to_apply=%add | all-reduce | flops 1536 | bytes 6144
  38.0 36.5 %all_gather.24 = bf16[768,3,192]{2,1,0:T(4,128)(2,1)S(1)} all-gather(bf16[96,3,192]{2,1,0:T(4,128)(2,1)S(1)} %copy.63), channel_id=1, replica_groups=mesh['dp'=2,'seq'=4,'tensor'=4] {'dp','seq'}, dimensions={0}, use_global_device_ids=true | all-gather | bytes 995328 | tf_op jit(solution)/shard_map/all_gather | solution.py:129
  76.0 8.5 %all_gather.22 = s32[2,512]{1,0:T(2,128)S(1)} all-gather(s32[2,128]{1,0:T(2,128)S(1)} %copy-done.61), channel_id=1, replica_groups=mesh['dp'=2,'seq'=4,'tensor'=4] {'seq'}, dimensions={1}, use_global_device_ids=true | all-gather | bytes 5120 | tf_op jit(solution)/shard_map/all_gather | solution.py:109
  85.4 13.0 %all_gather.25 = bf16[3,512,64]{1,2,0:T(8,128)(2,1)S(1)} all-gather(bf16[3,128,64]{1,2,0:T(8,128)(2,1)S(1)} %get-tuple-element.508), channel_id=1, replica_groups=mesh['dp'=2,'seq'=4,'tensor'=4] {'seq'}, dimensions={1}, use_global_device_ids=true | all-gather | bytes 245760 | tf_op jit(solution)/shard_map/all_gather | solution.py:151
  99.5 12.6 %all_gather.26 = bf16[3,512,64]{1,2,0:T(8,128)(2,1)S(1)} all-gather(bf16[3,128,64]{1,2,0:T(8,128)(2,1)S(1)} %fusion.168), channel_id=1, replica_groups=mesh['dp'=2,'seq'=4,'tensor'=4] {'seq'}, dimensions={1}, use_global_device_ids=true | all-gather | bytes 245760 | tf_op jit(solution)/shard_map/all_gather | solution.py:152
  113.7 7.8 %while.52 = (s32[]{:T(128)}, bf16[3,128,64]{1,2,0:T(8,128)(2,1)S(1)}, f32[3,128]{1,0:T(4,128)S(1)}, s32[128]{0:T(128)S(1)}, s32[512]{0:T(512)S(1)}, /*index=5*/b...) while((s32[]{:T(128)}, ...), condition=%wide.region_5.6_spmd, body=%wide.region_2.5_spmd.sunk | while | flops 17309568 | bytes 1107049 | solution.py:154
  123.4 31.8 %all_gather.27 = bf16[192,768]{0,1:T(8,128)(2,1)S(1)} all-gather(bf16[192,96]{0,1:T(8,128)(2,1)S(1)} %copy.68), channel_id=1, replica_groups=mesh['dp'=2,'seq'=4,'tensor'=4] {'dp','seq'}, dimensions={1}, use_global_device_ids=true | all-gather | bytes 331776 | tf_op jit(solution)/shard_map/all_gather | solution.py:130
  155.9 12.5 %all_gather.60 = bf16[3,512,64]{1,2,0:T(8,128)(2,1)S(1)} all-gather(bf16[3,128,64]{1,2,0:T(8,128)(2,1)S(1)} %get-tuple-element.510), channel_id=1, replica_groups=mesh['dp'=2,'seq'=4,'tensor'=4] {'seq'}, dimensions={1}, use_global_device_ids=true | all-gather | bytes 245760 | tf_op jit(solution)/shard_map/all_gather | solution.py:151
  168.8 12.6 %all_gather.61 = bf16[3,512,64]{1,2,0:T(8,128)(2,1)S(1)} all-gather(bf16[3,128,64]{1,2,0:T(8,128)(2,1)S(1)} %fusion.169), channel_id=1, replica_groups=mesh['dp'=2,'seq'=4,'tensor'=4] {'seq'}, dimensions={1}, use_global_device_ids=true | all-gather | bytes 245760 | tf_op jit(solution)/shard_map/all_gather | solution.py:152
  181.6 4.4 while.53
  188.3 35.1 %all_gather.58 = bf16[768,2,288]{2,0,1:T(8,128)(2,1)S(1)} all-gather(bf16[96,2,288]{2,0,1:T(8,128)(2,1)S(1)} %copy.69), channel_id=1, replica_groups=mesh['dp'=2,'seq'=4,'tensor'=4] {'dp','seq'}, dimensions={0}, use_global_device_ids=true | all-gather | bytes 995328 | tf_op jit(solution)/shard_map/all_gather | solution.py:131
  225.5 32.2 %all_gather.59 = bf16[288,768]{0,1:T(8,128)(2,1)S(1)} all-gather(bf16[288,96]{0,1:T(8,128)(2,1)} %copy.71), channel_id=1, replica_groups=mesh['dp'=2,'seq'=4,'tensor'=4] {'dp','seq'}, dimensions={1}, use_global_device_ids=true | all-gather | bytes 497664 | tf_op jit(solution)/shard_map/all_gather | solution.py:132
  264.9 33.5 %all-reduce.15.cloned.1.call-done = (f32[128,768]{1,0:T(8,128)}, f32[128,768]{1,0:T(8,128)}) async-done(((f32[128,768]{1,0:T(8,128)}, f32[128,768]{1,0:T(8,128)}), (f32[128,768]{1,0:T(8,128)}, f32[128,768]{1,0:T(8,128)})) %all-reduce.15.cloned.1.call-update) | async-done | bytes 786448 | tf_op jit(solution)/shard_map/psum | solution.py:89
  298.5 2.1 multiply_reduce_fusion.1
  300.6 2.4 bitcast_add_fusion.1
  305.6 1.6 multiply_reduce_fusion.17
  309.3 21.2 %while.54 = (s32[]{:T(128)}, f32[3,128,64]{1,2,0:T(8,128)}, bf16[3,512,64]{1,2,0:T(8,128)(2,1)}, bf16[3,512,64]{1,2,0:T(8,128)(2,1)}, s32[128]{0:T(128)}, /*inde...) while((s32[]{:T(128)}, f32[3,128,64]{1,2,0:T(8,128)}, ...), condition=%wide.region_25.26_spmd, body=%wide.region_24.25_spmd.sunk | while | flops 42532864 | bytes 2009729 | solution.py:227
  313.8 1.7 fusion.283
  320.9 1.7 fusion.283
  327.9 1.7 fusion.283
  330.5 2.0 copy.100
  332.5 2.1 reshape.360
  336.4 2.0 copy.102
  338.4 2.1 reshape.362
  340.5 1.9 convolution_convert_fusion.2
  346.6 19.0 %while.55 = (s32[]{:T(128)}, f32[3,128,64]{1,2,0:T(8,128)}, bf16[3,512,64]{1,2,0:T(8,128)(2,1)}, bf16[3,512,64]{1,2,0:T(8,128)(2,1)}, s32[128]{0:T(128)}, /*inde...) while((s32[]{:T(128)}, f32[3,128,64]{1,2,0:T(8,128)}, ...), condition=%wide.region_36.37_spmd, body=%wide.region_35.36_spmd.sunk | while | flops 42532864 | bytes 2009729 | solution.py:227
  350.3 1.7 fusion.299
  356.7 1.7 fusion.299
  363.0 1.7 fusion.299
  365.6 2.0 copy.104
  367.6 2.1 reshape.364
  369.8 2.1 fusion.154
  378.3 17.8 %reduce-scatter.29.cloned.1.call-done = bf16[128,192]{1,0:T(8,128)(2,1)} async-done(((bf16[512,192]{1,0:T(8,128)(2,1)}), bf16[128,192]{1,0:T(8,128)(2,1)}) %reduce-scatter.29.cloned.1.call-update) | async-done | bytes 49168
  399.4 17.7 %reduce-scatter.31.cloned.1.call-done = bf16[128,192]{1,0:T(8,128)(2,1)} async-done(((bf16[512,192]{1,0:T(8,128)(2,1)}), bf16[128,192]{1,0:T(8,128)(2,1)}) %reduce-scatter.31.cloned.1.call-update) | async-done | bytes 49168
  423.1 1.9 convolution_add_fusion.3
  425.0 2.2 copy.108
  429.8 2.6 copy.110
  433.3 2.0 convolution_add_fusion
  436.9 2.0 convolution_add_fusion.1
  439.6 24.5 %all-reduce.13.cloned.1.call-done = (f32[128,768]{1,0:T(8,128)}, f32[128,768]{1,0:T(8,128)}, f32[128,768]{1,0:T(8,128)}, f32[128,768]{1,0:T(8,128)}) async-done(((f32[128,768]{1,0:T(8,128)}, f32[128,768]{1,0:T(8,128)}, f32[128,768]{1,0:T(8,128)}, f32[128,768]{1,0:T(8,128)}), (f32[128,768]{1,0:T(8,128)}, f32[128,768]{1,0:T(8,128)}, f32[128,768]{1,0:T(8,128)}, ...) | async-done | bytes 1572880 | tf_op jit(solution)/shard_map/psum | solution.py:89
  465.6 22.0 %all-reduce.4 = (f32[768]{0:T(1024)S(1)}, f32[768]{0:T(1024)S(1)}) all-reduce(f32[768]{0:T(1024)S(1)} %add.236, f32[768]{0:T(1024)S(1)} %add.237), channel_id=10, replica_groups=mesh['dp'=2,'seq'=4,'tensor'=4] {'dp','seq'}, use_global_device_ids=true, to_apply=%region_48.49.clone | all-reduce | flops 1536 | bytes 12288
  488.8 42.6 %reduce-scatter.33.cloned.1.call-done = f32[96,192]{1,0:T(8,128)} async-done(((f32[768,192]{1,0:T(8,128)}), f32[96,192]{1,0:T(8,128)}) %reduce-scatter.33.cloned.1.call-update) | async-done | bytes 73744
  531.4 1.6 copy.109
  536.5 61.9 %reduce-scatter.35.cloned.1.call-done = f32[96,288]{1,0:T(8,128)} async-done(((f32[768,288]{1,0:T(8,128)}), f32[96,288]{1,0:T(8,128)}) %reduce-scatter.35.cloned.1.call-update) | async-done | bytes 110608
  598.5 1.7 copy.111
  600.2 70.3 %reduce-scatter.23.cloned.1.call-done = f32[96,2,288]{2,0,1:T(8,128)} async-done(((f32[768,2,288]{2,0,1:T(8,128)}), f32[96,2,288]{2,0,1:T(8,128)}) %reduce-scatter.23.cloned.1.call-update) | async-done | bytes 221200 | tf_op jit(solution)/shard_map/reduce_scatter | solution.py:266
  670.5 1.9 copy.89
  672.4 70.9 %reduce-scatter.21.cloned.1.call-done = f32[96,3,192]{2,0,1:T(8,128)} async-done(((f32[768,3,192]{2,0,1:T(8,128)}), f32[96,3,192]{2,0,1:T(8,128)}) %reduce-scatter.21.cloned.1.call-update) | async-done | bytes 221200 | tf_op jit(solution)/shard_map/reduce_scatter | solution.py:264
  (347 shorter events, 104.9 us)
Async XLA Ops:
  7.2 250.6 %all-reduce.17.cloned.1.call-start = ((), (), s32[]{:S(2)}) async-start(), calls=%async_computation.18 | async-start | bytes 1572864 | tf_op jit(solution)/shard_map/psum | solution.py:89
  8.5 67.0 %copy-start.51 = (f32[128]{0:T(128)}, f32[128]{0:T(128)S(1)}, u32[]{:S(2)}) copy-start(f32[128]{0:T(128)S(1)} %get-tuple-element.558) | copy-start | bytes 1540
  8.5 76.1 %copy-start.49 = (f32[128]{0:T(128)}, f32[128]{0:T(128)S(1)}, u32[]{:S(2)}) copy-start(f32[128]{0:T(128)S(1)} %get-tuple-element.557) | copy-start | bytes 1540
  9.8 65.6 %copy-start = (f32[2,128,768]{2,1,0:T(8,128)S(1)}, f32[2,128,768]{2,1,0:T(8,128)}, u32[]{:S(2)}) copy-start(f32[2,128,768]{2,1,0:T(8,128)} %param.17) | copy-start | bytes 2359300
  9.9 66.1 %copy-start.66 = (f32[128]{0:T(128)}, f32[128]{0:T(128)S(1)}, u32[]{:S(2)}) copy-start(f32[128]{0:T(128)S(1)} %add_rsqrt_fusion.3) | copy-start | bytes 1540
  84.6 28.5 %copy-start.62 = (f32[128]{0:T(128)}, f32[128]{0:T(128)S(1)}, u32[]{:S(2)}) copy-start(f32[128]{0:T(128)S(1)} %add_rsqrt_fusion.1) | copy-start | bytes 1540
  85.3 28.3 %copy-start.38 = (f32[128,64]{0,1:T(8,128)}, f32[128,64]{0,1:T(8,128)S(1)}, u32[]{:S(2)}) copy-start(f32[128,64]{0,1:T(8,128)S(1)} %get-tuple-element.560) | copy-start | bytes 98308
  85.3 28.3 %copy-start.41 = (f32[128,64]{0,1:T(8,128)}, f32[128,64]{0,1:T(8,128)S(1)}, u32[]{:S(2)}) copy-start(f32[128,64]{0,1:T(8,128)S(1)} %get-tuple-element.559) | copy-start | bytes 98308
  113.6 9.6 %copy-start.47 = (bf16[192,96]{1,0:T(8,128)(2,1)S(1)}, bf16[192,96]{1,0:T(8,128)(2,1)}, u32[]{:S(2)}) copy-start(bf16[192,96]{1,0:T(8,128)(2,1)} %param.20) | copy-start | bytes 110596
  123.2 140.9 %copy-start.26 = (bf16[3,128,64]{1,2,0:T(8,128)(2,1)}, bf16[3,128,64]{1,2,0:T(8,128)(2,1)S(1)}, u32[]{:S(2)}) copy-start(bf16[3,128,64]{1,2,0:T(8,128)(2,1)S(1)} %get-tuple-element.222) | copy-start | bytes 147460
  155.2 32.0 %copy-start.3 = (bf16[192,768]{0,1:T(8,128)(2,1)}, bf16[192,768]{0,1:T(8,128)(2,1)S(1)}, u32[]{:S(2)}) copy-start(bf16[192,768]{0,1:T(8,128)(2,1)S(1)} %all_gather.27) | copy-start | bytes 884740
  186.1 38.7 %copy-start.14 = (bf16[3,128,64]{2,1,0:T(8,128)(2,1)}, bf16[3,128,64]{2,1,0:T(8,128)(2,1)S(1)}, u32[]{:S(2)}) copy-start(bf16[3,128,64]{2,1,0:T(8,128)(2,1)S(1)} %get-tuple-element.996) | copy-start | bytes 147460
  186.1 38.7 %copy-start.25 = (bf16[3,128,64]{1,2,0:T(8,128)(2,1)}, bf16[3,128,64]{1,2,0:T(8,128)(2,1)S(1)}, u32[]{:S(2)}) copy-start(bf16[3,128,64]{1,2,0:T(8,128)(2,1)S(1)} %get-tuple-element.223) | copy-start | bytes 147460
  186.1 38.7 %copy-start.60 = (f32[3,128]{1,0:T(4,128)}, f32[3,128]{1,0:T(4,128)S(1)}, u32[]{:S(2)}) copy-start(f32[3,128]{1,0:T(4,128)S(1)} %get-tuple-element.891) | copy-start | bytes 4612
  188.2 36.6 %copy-start.46 = (bf16[288,96]{1,0:T(8,128)(2,1)S(1)}, bf16[288,96]{1,0:T(8,128)(2,1)}, u32[]{:S(2)}) copy-start(bf16[288,96]{1,0:T(8,128)(2,1)} %param.22) | copy-start | bytes 165892
  188.2 110.2 %all-reduce.15.cloned.1.call-start = ((), (), s32[]{:S(2)}) async-start(), calls=%async_computation.17 | async-start | bytes 1572864 | tf_op jit(solution)/shard_map/psum | solution.py:89
  223.4 34.3 %copy-start.1 = (bf16[768,2,288]{2,0,1:T(8,128)(2,1)}, bf16[768,2,288]{2,0,1:T(8,128)(2,1)S(1)}, u32[]{:S(2)}) copy-start(bf16[768,2,288]{2,0,1:T(8,128)(2,1)S(1)} %all_gather.58) | copy-start | bytes 2654212
  259.1 41.5 %copy-start.57 = (f32[128]{0:T(128)}, f32[128]{0:T(128)S(1)}, u32[]{:S(2)}) copy-start(f32[128]{0:T(128)S(1)} %broadcast_multiply_fusion.10) | copy-start | bytes 1540
  259.3 41.3 %copy-start.68 = (f32[128]{0:T(128)}, f32[128]{0:T(128)S(1)}, u32[]{:S(2)}) copy-start(f32[128]{0:T(128)S(1)} %add_rsqrt_fusion.2) | copy-start | bytes 1540
  259.3 41.3 %copy-start.55 = (f32[128]{0:T(128)}, f32[128]{0:T(128)S(1)}, u32[]{:S(2)}) copy-start(f32[128]{0:T(128)S(1)} %broadcast_multiply_fusion.8) | copy-start | bytes 1540
  259.6 41.1 %copy-start.64 = (f32[128]{0:T(128)}, f32[128]{0:T(128)S(1)}, u32[]{:S(2)}) copy-start(f32[128]{0:T(128)S(1)} %add_rsqrt_fusion) | copy-start | bytes 1540
  260.0 2.7 copy-start.19
  260.6 3.6 copy-start.16
  261.3 37.1 %copy-start.28 = (bf16[128,1,288]{0,2,1:T(8,128)(2,1)}, bf16[128,1,288]{0,2,1:T(8,128)(2,1)S(1)}, u32[]{:S(2)}) copy-start(bf16[128,1,288]{0,2,1:T(8,128)(2,1)S(1)} %get-tuple-element.506) | copy-start | bytes 221188
  264.1 111.2 %reduce-scatter.25.cloned.1.call-start = ((), (), s32[]{:S(2)}) async-start(), calls=%async_computation.10 | async-start | bytes 327680
  298.4 5.3 copy-start.4
  332.5 14.1 %copy-start.15 = (bf16[3,128,64]{2,1,0:T(8,128)(2,1)S(1)}, bf16[3,128,64]{2,1,0:T(8,128)(2,1)}, u32[]{:S(2)}) copy-start(bf16[3,128,64]{2,1,0:T(8,128)(2,1)} %copy-done.14) | copy-start | bytes 147460
  334.7 42.6 %reduce-scatter.27.cloned.1.call-start = ((), (), s32[]{:S(2)}) async-start(), calls=%async_computation.11 | async-start | bytes 327680
  343.4 52.7 %reduce-scatter.29.cloned.1.call-start = ((), (), s32[]{:S(2)}) async-start(), calls=%async_computation.12 | async-start | bytes 327680
  365.6 6.3 copy-start.17
  369.7 6.7 copy-start.24
  369.7 47.3 %reduce-scatter.31.cloned.1.call-start = ((), (), s32[]{:S(2)}) async-start(), calls=%async_computation.13 | async-start | bytes 327680
  373.0 24.2 %copy-start.40 = (f32[128,64]{0,1:T(8,128)S(1)}, f32[128,64]{0,1:T(8,128)}, u32[]{:S(2)}) copy-start(f32[128,64]{0,1:T(8,128)} %copy-done.39) | copy-start | bytes 98308
  373.0 45.7 %copy-start.42 = (f32[128,64]{0,1:T(8,128)S(1)}, f32[128,64]{0,1:T(8,128)}, u32[]{:S(2)}) copy-start(f32[128,64]{0,1:T(8,128)} %copy-done.41) | copy-start | bytes 98308
  375.3 88.8 %all-reduce.13.cloned.1.call-start = ((), (), s32[]{:S(2)}) async-start(), calls=%async_computation.16 | async-start | bytes 3145728 | tf_op jit(solution)/shard_map/psum | solution.py:89
  418.8 4.1 copy-start.11
  418.8 4.1 copy-start.27
  419.9 3.2 copy-start.12
  422.8 4.5 copy-start.9
  422.8 108.6 %reduce-scatter.33.cloned.1.call-start = ((), (), s32[]{:S(2)}) async-start(), calls=%async_computation.14 | async-start | bytes 884736
  423.1 5.4 copy-start.18
  427.3 171.2 %reduce-scatter.35.cloned.1.call-start = ((), (), s32[]{:S(2)}) async-start(), calls=%async_computation.15 | async-start | bytes 1327104
  428.6 3.9 copy-start.33
  428.6 3.9 copy-start.58
  428.6 3.9 copy-start.69
  429.8 2.7 copy-start.35
  432.4 238.1 %reduce-scatter.23.cloned.1.call-start = ((), (), s32[]{:S(2)}) async-start(), calls=%async_computation.9 | async-start | bytes 2654208 | tf_op jit(solution)/shard_map/reduce_scatter | solution.py:266
  435.4 308.0 %reduce-scatter.21.cloned.1.call-start = ((), (), s32[]{:S(2)}) async-start(), calls=%async_computation.8 | async-start | bytes 2654208 | tf_op jit(solution)/shard_map/reduce_scatter | solution.py:264
  (33 other events, 44.1 us)
Sparse Core Ops, SparseCore 0:
  188.3 35.4 all-reduce.16
  264.3 34.1 all-reduce.14
  334.8 19.9 reduce-scatter.24
  356.9 18.2 reduce-scatter.26
  377.9 18.1 reduce-scatter.28
  398.8 18.2 reduce-scatter.30
  422.9 41.1 all-reduce.12
  468.0 63.3 reduce-scatter.32
  534.8 63.6 reduce-scatter.34
  601.8 68.6 reduce-scatter.22
  674.6 68.7 reduce-scatter.20
where the time goes:
time: 752 us; the launch traced here: 750 us
  waiting for transfers between devices  339 us (45%)
  blocking collectives  240 us (32%)
  matrix products  72 us (10%)
  local copies, waits for them, and re-layouts  58.2 us (8%)
  other arithmetic  22.7 us (3%)
  between operations  16.4 us (2%)
    unnamed x17, waiting for transfers between devices  140 us
    reduce_scatter x1, waiting for transfers between devices, per_device(): lax.psum_scatter(g_qkv, ('dp', 'seq'), scatter_dimension=0, tiled=True)  70.9 us
    reduce_scatter x1, waiting for transfers between devices, per_device(): lax.psum_scatter(g_mlp_in, ('dp', 'seq'), scatter_dimension=0, tiled=True)  70.3 us
    psum x3, waiting for transfers between devices, tensor_total(): return lax.psum(partial_sum, 'tensor')  58 us
    unnamed x2, blocking collectives  45.3 us
    unnamed x172, local copies, waits for them, and re-layouts  40.8 us
    all_gather x1, blocking collectives, per_device(): lax.all_gather(shards[0], ('dp', 'seq'), axis=0, tiled=True)  36.5 us
    all_gather x1, blocking collectives, per_device(): lax.all_gather(shards[2], ('dp', 'seq'), axis=0, tiled=True)  35.1 us
  transfers between devices with their start and end apart: 11, of which 8 were waited for; matrix products, arithmetic and copies ran while one was open for 10% of the time, Pallas kernels for 0%

commit v1 on v0

v1 whole, which is shorter than its diff:
```python
import math

import jax
import jax.numpy as jnp
from jax import lax
from jax.experimental import pallas as pl
from jax.experimental.pallas import tpu as pltpu
from jax.sharding import PartitionSpec as P

D = 768
HD = 64
EPS = 1e-05
ROPE_BASE = 160000.0
INV_ROOT2 = 0.7071067811865476
INV_ROOT2PI = 0.3989422804014327
MESH = pl.DeviceIdType.MESH
BF = jnp.bfloat16
F32 = jnp.float32
VM = pl.BlockSpec(memory_space=pltpu.VMEM)


def layer_norm(values):
    mean = jnp.mean(values, axis=-1, keepdims=True)
    centred = values - mean
    inverse = lax.rsqrt(jnp.mean(centred * centred, axis=-1, keepdims=True) + EPS)
    return centred * inverse, inverse


def norm_backward(e, xhat, r):
    first = jnp.mean(e, axis=-1, keepdims=True)
    second = jnp.mean(e * xhat, axis=-1, keepdims=True)
    return r * (e - first - xhat * second)


def rope_tables(places):
    half = HD // 2
    ramp = jnp.arange(half, dtype=F32) * (2.0 / HD)
    freq = jnp.exp(-math.log(ROPE_BASE) * ramp)
    angle = places.astype(F32)[:, None] * freq[None, :]
    cosine, sine = jnp.cos(angle), jnp.sin(angle)
    return jnp.concatenate([cosine, cosine], axis=-1), jnp.concatenate([sine, sine], axis=-1)


def rotate(values, cosine, sine):
    half = HD // 2
    turned = jnp.concatenate([-values[..., half:], values[..., :half]], axis=-1)
    return values * cosine[:, None, :] + turned * sine[:, None, :]


def unrotate(grads, cosine, sine):
    half = HD // 2
    moved = grads * sine[:, None, :]
    back = jnp.concatenate([moved[..., half:], -moved[..., :half]], axis=-1)
    return grads * cosine[:, None, :] + back


def gelu_parts(a):
    cdf = 0.5 * (1.0 + lax.erf(a * INV_ROOT2))
    return a * cdf, cdf + a * jnp.exp(-0.5 * a * a) * INV_ROOT2PI


def greet(axis, n):
    me = lax.axis_index(axis)
    barrier = pltpu.get_barrier_semaphore()
    for step in range(1, n):
        pl.semaphore_signal(
            barrier, inc=1, device_id={axis: lax.rem(me + step, n)}, device_id_type=MESH
        )
    pl.semaphore_wait(barrier, n - 1)
    return me


def push(src, dst, send, recv, axis, peer):
    copy = pltpu.make_async_remote_copy(
        src_ref=src, dst_ref=dst, send_sem=send, recv_sem=recv,
        device_id={axis: peer}, device_id_type=MESH,
    )
    copy.start()
    return copy


def gather_blocks(arrays, axis, n, cid):
    count = len(arrays)

    def kernel(*refs):
        ins, outs = refs[:count], refs[count : 2 * count]
        send, recv, local = refs[2 * count :]
        me = greet(axis, n)
        copies = []
        for i in range(count):
            for step in range(1, n):
                copies.append(
                    push(ins[i], outs[i].at[me], send.at[i, step], recv.at[i, step], axis,
                         lax.rem(me + step, n))
                )
        for i in range(count):
            own = pltpu.make_async_copy(ins[i], outs[i].at[me], local.at[i])
            own.start()
            own.wait()
        for copy in copies:
            copy.wait()

    return pl.pallas_call(
        kernel,
        out_shape=[jax.ShapeDtypeStruct((n,) + a.shape, a.dtype) for a in arrays],
        in_specs=[VM] * count,
        out_specs=[VM] * count,
        scratch_shapes=[
            pltpu.SemaphoreType.DMA((count, n)),
            pltpu.SemaphoreType.DMA((count, n)),
            pltpu.SemaphoreType.DMA((count,)),
        ],
        compiler_params=pltpu.CompilerParams(collective_id=cid, has_side_effects=True),
    )(*arrays)


def scatter_sum(blocks, axis, n, cid):
    shape = blocks.shape[1:]

    def kernel(in_ref, out_ref, land, send, recv):
        me = greet(axis, n)
        copies = [
            push(in_ref.at[lax.rem(me + step, n)], land.at[step - 1], send.at[step],
                 recv.at[step], axis, lax.rem(me + step, n))
            for step in range(1, n)
        ]
        total = in_ref[me].astype(F32)
        for step, copy in enumerate(copies):
            copy.wait()
            total = total + land[step].astype(F32)
        out_ref[...] = total

    return pl.pallas_call(
        kernel,
        out_shape=jax.ShapeDtypeStruct(shape, F32),
        in_specs=[VM],
        out_specs=VM,
        scratch_shapes=[
            pltpu.VMEM((n - 1,) + shape, blocks.dtype),
            pltpu.SemaphoreType.DMA((n,)),
            pltpu.SemaphoreType.DMA((n,)),
        ],
        compiler_params=pltpu.CompilerParams(collective_id=cid, has_side_effects=True),
    )(blocks)


def sum_rows_then_gather(partials, extras, middle, gathered, owned, axis, n, cid):
    np_, ne, ng, no = len(partials), len(extras), len(gathered), len(owned)
    rows = partials[0].shape[1:]

    def kernel(*refs):
        refs = list(refs)
        take = lambda k: [refs.pop(0) for _ in range(k)]
        parts, more, gouts, oouts, lands = take(np_), take(ne), take(ng), take(no), take(np_)
        send, recv, gsend, grecv = refs
        me = greet(axis, n)
        copies = []
        for i in range(np_):
            copies.append([
                push(parts[i].at[lax.rem(me + step, n)], lands[i].at[step - 1], send.at[i, step],
                     recv.at[i, step], axis, lax.rem(me + step, n))
                for step in range(1, n)
            ])
        sums = []
        for i in range(np_):
            total = parts[i][me].astype(F32)
            for step, copy in enumerate(copies[i]):
                copy.wait()
                total = total + lands[i][step].astype(F32)
            sums.append(total)
        shared, kept = middle(sums, [m[...] for m in more])
        copies = []
        for i in range(ng):
            gouts[i][me] = shared[i].astype(gathered[i][1])
            for step in range(1, n):
                copies.append(
                    push(gouts[i].at[me], gouts[i].at[me], gsend.at[i, step], grecv.at[i, step],
                         axis, lax.rem(me + step, n))
                )
        for i in range(no):
            oouts[i][...] = kept[i].astype(owned[i][1])
        for copy in copies:
            copy.wait()

    return pl.pallas_call(
        kernel,
        out_shape=[jax.ShapeDtypeStruct((n,) + s, t) for s, t in gathered]
        + [jax.ShapeDtypeStruct(s, t) for s, t in owned],
        in_specs=[VM] * (np_ + ne),
        out_specs=[VM] * (ng + no),
        scratch_shapes=[pltpu.VMEM((n - 1,) + rows, p.dtype) for p in partials]
        + [
            pltpu.SemaphoreType.DMA((np_, n)),
            pltpu.SemaphoreType.DMA((np_, n)),
            pltpu.SemaphoreType.DMA((ng, n)),
            pltpu.SemaphoreType.DMA((ng, n)),
        ],
        compiler_params=pltpu.CompilerParams(collective_id=cid, has_side_effects=True),
    )(*partials, *extras)


def dot(a, b):
    return jnp.dot(a, b, preferred_element_type=F32)


def dot_t(a, b):
    return lax.dot_general(a, b, (((1,), (1,)), ((), ())), preferred_element_type=F32)


def t_dot(a, b):
    return lax.dot_general(a, b, (((0,), (0,)), ((), ())), preferred_element_type=F32)


def make_per_device(mesh):
    n_seq, n_ten = mesh.shape["seq"], mesh.shape["tensor"]

    def per_device(tokens, positions, qkv_weight, attn_out_weight, mlp_in_weight, mlp_out_weight,
                   attn_gain, mlp_gain, cotangent):
        S, R = tokens.shape[:2]
        T, L = S * R, R * n_seq
        w, u = qkv_weight.shape[2], mlp_out_weight.shape[0]
        h = w // HD
        wr = qkv_weight.shape[0]
        own = T // n_ten
        group = ("dp", "seq")
        pack_a = jnp.concatenate(
            [qkv_weight.reshape(wr, 3 * w), attn_gain[:, None], mlp_gain[:, None]], axis=1)
        pack_b = jnp.concatenate(
            [attn_out_weight.T, mlp_in_weight.reshape(wr, 2 * u), mlp_out_weight.T], axis=1)
        full_a = lax.all_gather(pack_a, group, axis=0, tiled=True)
        full_b = lax.all_gather(pack_b, group, axis=0, tiled=True)
        w_qkv = full_a[:, : 3 * w]
        gain1 = full_a[:, 3 * w].astype(F32)[None, :]
        gain2 = full_a[:, 3 * w + 1].astype(F32)[None, :]
        w_out_t = full_b[:, :w]
        w_in = full_b[:, w : w + 2 * u]
        w_down_t = full_b[:, w + 2 * u :]

        x = tokens.reshape(T, D)
        cot = cotangent.reshape(T, D)
        dyb = cot.astype(BF)
        t_me = lax.axis_index("tensor")
        mine = lambda a: lax.dynamic_slice_in_dim(a, t_me * own, own, 0)
        x_own, cot_own = mine(x), mine(cot)

        index = lax.axis_index("seq") * R + jnp.arange(R, dtype=jnp.int32)
        starts = index[None, :] - positions
        cosine, sine = rope_tables(positions.reshape(T))

        xhat1, _ = layer_norm(x)
        normed1 = (xhat1 * gain1).astype(BF)
        qkv = dot(normed1, w_qkv).reshape(T, 3, h, HD)
        q = rotate(qkv[:, 0], cosine, sine).astype(BF)
        k = rotate(qkv[:, 1], cosine, sine).astype(BF)
        v = qkv[:, 2].astype(BF)
        kv = jnp.concatenate([k.reshape(T, w), v.reshape(T, w)], axis=1)
        starts8 = jnp.pad(starts, ((0, 8 - S), (0, 0)))
        kv_all, starts_all = gather_blocks([kv, starts8], "seq", n_seq, 0)
        k_start = jnp.transpose(starts_all[:, :S], (1, 0, 2)).reshape(S, L)
        kv_heads = jnp.transpose(
            kv_all.reshape(n_seq, S, R, 2, h, HD), (3, 1, 4, 0, 2, 5)).reshape(2, S, h, L, HD)
        keys, values = kv_heads[0], kv_heads[1]
        qh = jnp.transpose(q.reshape(S, R, h, HD), (0, 2, 1, 3))
        scale = 1.0 / math.sqrt(HD)
        mask = (starts[:, :, None] == k_start[:, None, :])[:, None]
        scores = jnp.einsum("shqd,shkd->shqk", qh, keys, preferred_element_type=F32) * scale
        scores = jnp.where(mask, scores, -jnp.inf)
        top = jnp.max(scores, axis=-1, keepdims=True)
        lse = top + jnp.log(jnp.sum(jnp.exp(scores - top), axis=-1, keepdims=True))
        probs32 = jnp.exp(scores - lse)
        probs = probs32.astype(BF)
        ctx_h = jnp.einsum("shqk,shkd->shqd", probs, values, preferred_element_type=F32).astype(BF)
        context = jnp.transpose(ctx_h, (0, 2, 1, 3)).reshape(T, w)

        mid_part = dot_t(context, w_out_t).astype(BF).reshape(n_ten, own, D)

        def after_attention(sums, more):
            mid = more[0] + sums[0]
            xhat2, _ = layer_norm(mid)
            return [xhat2 * more[1]], [mid]

        normed2, mid_own = sum_rows_then_gather(
            [mid_part], [x_own, gain2], after_attention,
            [((own, D), BF)], [((own, D), F32)], "tensor", n_ten, 1)
        normed2 = normed2.reshape(T, D)
        up = dot(normed2, w_in)
        active, slope = gelu_parts(up[:, :u])
        gate = up[:, u:]
        hidden = (active * gate).astype(BF)
        out_part = dot_t(hidden, w_down_t).astype(BF).reshape(n_ten, own, D)
        dhidden = dot(dyb, w_down_t)
        dup = jnp.concatenate([dhidden * gate * slope, dhidden * active], axis=1).astype(BF)
        dn2_part = dot_t(dup, w_in).astype(BF).reshape(n_ten, own, D)

        def after_mlp(sums, more):
            mid, dy, gain = more
            xhat2, rstd2 = layer_norm(mid)
            dn2, down = sums
            gain_grad = jnp.sum(dn2 * xhat2, axis=0, keepdims=True)
            dmid = dy + norm_backward(dn2 * gain, xhat2, rstd2)
            return [dmid, mid + down], [dmid, gain_grad]

        dmidb, out_rows, dmid_own, g_gain2 = sum_rows_then_gather(
            [dn2_part, out_part], [mid_own, cot_own, gain2], after_mlp,
            [((own, D), BF), ((own, D), BF)], [((own, D), F32), ((1, D), F32)],
            "tensor", n_ten, 2)
        output = out_rows.astype(F32).reshape(S, R, D)
        dmidb = dmidb.reshape(T, D)
        dcontext = dot(dmidb, w_out_t).astype(BF)
        g_b = jnp.concatenate([
            t_dot(dmidb, context).astype(BF),
            t_dot(normed2, dup).astype(BF),
            t_dot(dyb, hidden).astype(BF),
        ], axis=1)
        sum_b = lax.psum_scatter(g_b, group, scatter_dimension=0, tiled=True)

        dch = jnp.transpose(dcontext.reshape(S, R, h, HD), (0, 2, 1, 3))
        delta = jnp.sum(dch.astype(F32) * ctx_h.astype(F32), axis=-1, keepdims=True)
        dprobs = jnp.einsum("shqd,shkd->shqk", dch, values, preferred_element_type=F32)
        dscores = (probs32 * (dprobs - delta) * scale).astype(BF)
        dqh = jnp.einsum("shqk,shkd->shqd", dscores, keys, preferred_element_type=F32)
        dkh = jnp.einsum("shqk,shqd->shkd", dscores, qh, preferred_element_type=F32)
        dvh = jnp.einsum("shqk,shqd->shkd", probs, dch, preferred_element_type=F32)
        dkv = jnp.stack([dkh, dvh]).astype(BF).reshape(2, S, h, n_seq, R, HD)
        dkv = jnp.transpose(dkv, (3, 1, 4, 0, 2, 5)).reshape(n_seq, T, 2 * w)
        dkv_own = scatter_sum(dkv, "seq", n_seq, 3)
        dq = unrotate(jnp.transpose(dqh, (0, 2, 1, 3)).reshape(T, h, HD), cosine, sine)
        dk = unrotate(dkv_own[:, :w].reshape(T, h, HD), cosine, sine)
        dqkv = jnp.concatenate(
            [dq.reshape(T, w), dk.reshape(T, w), dkv_own[:, w:]], axis=1).astype(BF)
        dn1_part = dot_t(dqkv, w_qkv).astype(BF).reshape(n_ten, own, D)

        def at_the_end(sums, more):
            rows, dmid, gain, gain_grad2 = more
            xhat, rstd = layer_norm(rows)
            dn1 = sums[0]
            gain_grad1 = jnp.sum(dn1 * xhat, axis=0, keepdims=True)
            grad = dmid + norm_backward(dn1 * gain, xhat, rstd)
            pad = jnp.zeros((6, D), F32)
            return [jnp.concatenate([gain_grad1, gain_grad2, pad], axis=0), grad], []

        gains, grad_rows = sum_rows_then_gather(
            [dn1_part], [x_own, dmid_own, gain1, g_gain2], at_the_end,
            [((8, D), F32), ((own, D), BF)], [], "tensor", n_ten, 4)
        grad_tokens = grad_rows.astype(F32).reshape(S, R, D)
        gains = jnp.sum(gains[:, :2], axis=0)
        g_a = jnp.concatenate([t_dot(normed1, dqkv).astype(BF), gains.T.astype(BF)], axis=1)
        sum_a = lax.psum_scatter(g_a, group, scatter_dimension=0, tiled=True)
        sum_a, sum_b = sum_a.astype(F32), sum_b.astype(F32)
        return (
            output,
            grad_tokens,
            sum_a[:, : 3 * w].reshape(wr, 3, w),
            sum_b[:, :w].T,
            sum_b[:, w : w + 2 * u].reshape(wr, 2, u),
            sum_b[:, w + 2 * u :].T,
            sum_a[:, 3 * w],
            sum_a[:, 3 * w + 1],
        )

    return per_device


def solution(mesh):
    rows = P("dp", "seq", None)
    group = ("dp", "seq")
    weights = (P(group, None, "tensor"), P("tensor", group), P(group, None, "tensor"),
               P("tensor", group), P(group), P(group))
    return jax.shard_map(
        make_per_device(mesh), mesh=mesh,
        in_specs=(rows, P("dp", "seq")) + weights + (rows,),
        out_specs=(rows, rows) + weights,
        check_vma=False,
    )
```

time: 752 us -> 340 us (0.45)
  waiting for transfers between devices: 339 us -> 127 us
  blocking collectives: 240 us -> 43 us
  Pallas kernels: 0 us -> 90.9 us
  matrix products: 72 us -> 17 us
  local copies, waits for them, and re-layouts: 58.2 us -> 37.9 us
  other arithmetic: 22.7 us -> 8.47 us
    all_gather x9 -> x1, blocking collectives: 195 us -> 43 us  [per_device(): full_a = lax.all_gather(pack_a, group, axis=0, tiled=True)]
    reduce_scatter x2 -> x0, waiting for transfers between devices: 141 us -> none  [the longest x1 70.9 us: per_device(): lax.psum_scatter(g_qkv, ('dp', 'seq'), scatter_dimension=0, tiled=True)]
    pallas_call x0 -> x5, Pallas kernels: none -> 90.9 us  [the longest x3 51.4 us: sum_rows_then_gather(): pl.pallas_call(kernel, out_shape=[jax.ShapeDtypeStruct((n,) + s, t) for s...]
    psum x3 -> x0, waiting for transfers between devices: 58 us -> none  [tensor_total(): return lax.psum(partial_sum, 'tensor')]
    dot_general x66 -> x18, matrix products: 72 us -> 17 us  [the longest x4 6.13 us: dot_t(): lax.dot_general(a, b, (((1,), (1,)), ((), ())), preferred_element_type=F32)]
    unnamed x2 -> x0, blocking collectives: 45.3 us -> none
    unnamed x172 -> x73, local copies, waits for them, and re-layouts: 40.8 us -> 14.3 us
    unnamed x17 -> x5, waiting for transfers between devices: 140 us -> 127 us
  transfers between devices with their start and end apart: 11 -> 3, of which waited for: 8 -> 2; matrix products, arithmetic and copies ran while one was open for 10% -> 7% of each run, Pallas kernels for 0% -> 6%
where the time goes in v1:
time: 340 us; the launch traced here: 339 us
  waiting for transfers between devices  127 us (37%)
  Pallas kernels  90.9 us (27%)
  blocking collectives  43 us (13%)
  local copies, waits for them, and re-layouts  37.9 us (11%)
  matrix products  17 us (5%)
  between operations  14.7 us (4%)
  other arithmetic  8.47 us (2%)
    unnamed x5, waiting for transfers between devices  127 us
    pallas_call x3, Pallas kernels, sum_rows_then_gather(): pl.pallas_call(kernel, out_shape=[jax.ShapeDtypeStruct((n,) + s, t) for s...  51.4 us
    all_gather x1, blocking collectives, per_device(): full_a = lax.all_gather(pack_a, group, axis=0, tiled=True)  43 us
    pallas_call x1, Pallas kernels, gather_blocks(): pl.pallas_call(kernel, out_shape=[jax.ShapeDtypeStruct((n,) + a.shape, a....  20.6 us
    pallas_call x1, Pallas kernels, scatter_sum(): pl.pallas_call(kernel, out_shape=jax.ShapeDtypeStruct(shape, F32), in_spe...  18.9 us
    unnamed x73, local copies, waits for them, and re-layouts  14.3 us
  transfers between devices with their start and end apart: 3, of which 2 were waited for; matrix products, arithmetic and copies ran while one was open for 7% of the time, Pallas kernels for 6%

profile of v1, /device:TPU:0, one launch (start us, length us, event | category | flops | bytes accessed | tf_op | source)
XLA Modules:
  0.0 339.2 jit_solution(15869196184218312427)
XLA Ops:
  7.2 0.9 copy.125
  8.1 1.1 reshape.262
  9.2 1.0 copy.126
  10.2 0.8 concatenate.58
  11.1 1.1 copy.127
  12.2 0.7 pad_maximum_fusion.9
  13.0 43.0 %all_gather.7 = bf16[768,578]{1,0:T(8,128)(2,1)S(1)} all-gather(bf16[96,578]{1,0:T(8,128)(2,1)S(1)} %copy.128), channel_id=1, replica_groups=mesh['dp'=2,'seq'=4,'tensor'=4] {'dp','seq'}, dimensions={0}, use_global_device_ids=true | all-gather | bytes 998784 | tf_op jit(solution)/shard_map/all_gather | solution.py:230
  61.1 0.8 pad_maximum_fusion.4.refs_0_
  62.5 20.6 %shard_map.152 = (bf16[4,256,384]{2,1,0:T(8,128)(2,1)}, s32[4,8,128]{2,1,0:T(8,128)}) custom-call(bf16[256,384]{1,0:T(8,128)(2,1)} %pad_maximum_fusion.4.refs_0_, s32[8,128]{1,0:T(8,128)} %pad.4.refs_1_), custom_call_target="tpu_custom_call" | custom-call | tf_op jit(solution)/shard_map/pallas_call | solution.py:103
  83.1 1.4 copy.136
  84.7 0.8 fusion.41
  86.8 0.7 slice_bitcast_fusion.4
  90.6 0.7 copy.139
  92.0 0.8 copy.148
  92.8 0.7 constant_dynamic-slice_fusion.1.refs_1_
  93.5 1.6 constant_dynamic-slice_fusion.refs_3_
  95.1 2.2 convolution_convert_fusion.7
  97.3 13.7 %shard_map.153 = (bf16[4,64,768]{2,1,0:T(8,128)(2,1)}, f32[64,768]{1,0:T(8,128)}) custom-call(bf16[4,64,768]{2,1,0:T(8,128)(2,1)} %bitcast.159, f32[64,768]{1,0:T(8,128)} %constant_dynamic-slice_fusion.1.refs_1_, f32[1,768]{1,0:T(1,128)} %reshape.286.refs_2_.refs_4_), custom_call_target="tpu_custom_call" | custom-call | tf_op jit(solution)/shard_map/pallas_call | solution.py:185
  111.0 2.5 fusion.3
  114.7 1.2 convolution_convert_fusion.8
  115.8 1.5 convolution_convert_fusion.6
  117.4 23.2 %shard_map.154 = (bf16[4,64,768]{2,1,0:T(8,128)(2,1)}, bf16[4,64,768]{2,1,0:T(8,128)(2,1)}, f32[64,768]{1,0:T(8,128)}, f32[1,768]{1,0:T(1,128)}) custom-call(bf16[4,64,768]{2,1,0:T(8,128)(2,1)} %bitcast.182, bf16[4,64,768]{2,1,0:T(8,128)(2,1)} %bitcast.160, f32[64,768]{1,0:T(8,128)} %get-tuple-element.21.refs_2_, ...), custom_call_target="tpu_custom_call" | custom-call | tf_op jit(solution)/shard_map/pallas_call | solution.py:185
  140.6 1.5 convolution_convert_fusion.11
  142.1 1.2 convolution_convert_fusion.3
  143.3 1.1 stack.10
  144.5 1.2 copy.146
  145.6 1.6 multiply_convert_fusion
  148.2 1.1 maximum_bitcast_fusion
  149.9 1.2 copy.147.in_ref
  151.0 18.9 %shard_map.155 = f32[256,384]{1,0:T(8,128)} custom-call(bf16[4,256,384]{2,1,0:T(8,128)(2,1)} %copy.147.in_ref), custom_call_target="tpu_custom_call" | custom-call | tf_op jit(solution)/shard_map/pallas_call | solution.py:133
  169.9 1.8 slice.206
  173.4 0.7 copy-done.2
  174.2 1.3 convolution_convert_fusion.5
  175.4 14.5 %shard_map.156 = (f32[4,8,768]{2,1,0:T(8,128)}, bf16[4,64,768]{2,1,0:T(8,128)(2,1)}) custom-call(bf16[4,64,768]{2,1,0:T(8,128)(2,1)} %bitcast.178, f32[64,768]{1,0:T(8,128)} %constant_dynamic-slice_fusion.1.refs_1_, f32[64,768]{1,0:T(8,128)} %get-tuple-element.24.refs_2_, f32[1,768]{1,0:T(1,128)} %reshape.289.refs_3_, f32[1,768]{1,0:T(1,128)} %get-tuple-element.25.refs_4_), custom_call_target="tpu_custom_call" | custom-call | tf_op jit(solution)/shard_map/pallas_call | solution.py:185
  190.0 0.9 slice_reduce_fusion
  191.6 1.3 copy.154
  194.5 2.2 copy.156
  196.8 1.0 copy-done.24
  197.7 0.9 bitcast_convert_fusion.1
  198.7 0.9 bitcast_convert_fusion
  199.6 60.6 %reduce-scatter.7.cloned.1.call-done = bf16[96,578]{1,0:T(8,128)(2,1)} async-done(((bf16[768,578]{1,0:T(8,128)(2,1)}), bf16[96,578]{1,0:T(8,128)(2,1)}) %reduce-scatter.7.cloned.1.call-update) | async-done | bytes 110992
  260.2 1.0 copy.155
  261.3 0.9 copy.151
  262.7 66.6 %reduce-scatter.9.cloned.1.call-done = bf16[96,1056]{1,0:T(8,128)(2,1)} async-done(((bf16[768,1056]{1,0:T(8,128)(2,1)}), bf16[96,1056]{1,0:T(8,128)(2,1)}) %reduce-scatter.9.cloned.1.call-update) | async-done | bytes 202768
  329.2 1.1 copy.157
  330.4 0.6 slice_bitcast_fusion.2
  331.1 0.7 slice_bitcast_fusion.1
  331.7 0.9 copy.152
  (149 shorter events, 17.9 us)
Async XLA Ops:
  7.2 87.9 %all-gather.2.cloned.1.call-start = ((), (), s32[]{:S(2)}) async-start(), calls=%async_computation.2 | async-start | bytes 1990656 | tf_op jit(solution)/shard_map/all_gather | solution.py:231
  11.0 249.1 %reduce-scatter.7.cloned.1.call-start = ((), (), s32[]{:S(2)}) async-start(), calls=%async_computation.3 | async-start | bytes 1105920
  13.0 44.0 %copy-start = (f32[2,128,768]{2,1,0:T(8,128)S(1)}, f32[2,128,768]{2,1,0:T(8,128)}, u32[]{:S(2)}) copy-start(f32[2,128,768]{2,1,0:T(8,128)} %param.9) | copy-start | bytes 2359300
  56.0 0.9 copy-start.1
  58.8 1.3 copy-start.32
  60.3 0.6 copy-start.22
  60.3 31.6 %copy-start.13 = (f32[256,64]{0,1:T(8,128)}, f32[256,64]{0,1:T(8,128)S(1)}, u32[]{:S(2)}) copy-start(f32[256,64]{0,1:T(8,128)S(1)} %get-tuple-element.104) | copy-start | bytes 196612
  86.0 3.5 %copy-start.3 = (bf16[2,3,512,64]{2,3,1,0:T(8,128)(2,1)}, bf16[2,3,512,64]{2,3,1,0:T(8,128)(2,1)S(1)}, u32[]{:S(2)}) copy-start(bf16[2,3,512,64]{2,3,1,0:T(8,128)(2,1)S(1)} %squeeze.30) | copy-start | bytes 1179652
  87.7 0.7 copy-start.15
  90.0 0.6 copy-start.17
  95.1 18.5 %copy-start.10 = (f32[2,128,768]{2,1,0:T(8,128)S(1)}, f32[2,128,768]{2,1,0:T(8,128)}, u32[]{:S(2)}) copy-start(f32[2,128,768]{2,1,0:T(8,128)} %param.17) | copy-start | bytes 2359300
  111.0 2.6 copy-start.4
  114.0 0.7 copy-start.20
  114.0 3.3 copy-start.26
  114.0 3.3 copy-start.28
  140.6 2.7 copy-start.18
  142.1 2.4 copy-start.6
  145.6 1.6 copy-start.16
  147.2 1.0 copy-start.8
  169.9 2.2 slice-start
  169.9 2.3 copy-start.23
  172.0 0.8 copy-start.14
  172.3 1.0 copy-start.5
  172.3 1.1 copy-start.12
  172.9 1.3 copy-start.2
  172.9 1.2 copy-start.30
  174.2 16.7 %copy-start.31 = (f32[256]{0:T(256)S(1)}, f32[256]{0:T(256)}, u32[]{:S(2)}) copy-start(f32[256]{0:T(256)} %get-tuple-element.97) | copy-start | bytes 3076
  191.6 1.5 copy-start.7
  191.6 1.5 copy-start.19
  191.6 1.7 copy-start.9
  191.6 1.7 copy-start.27
  191.6 1.7 copy-start.29
  193.0 1.1 copy-start.11
  193.0 1.1 copy-start.21
  193.0 136.2 %reduce-scatter.9.cloned.1.call-start = ((), (), s32[]{:S(2)}) async-start(), calls=%async_computation.4 | async-start | bytes 1990656
  196.7 1.0 copy-start.24
  196.7 1.9 copy-start.25
Sparse Core Ops, SparseCore 0:
  11.2 58.3 all-gather.1
  193.1 67.0 reduce-scatter.6
  263.6 65.5 reduce-scatter.8

commit v2 on v1

--- a/solution.py
+++ b/solution.py
@@ -59,15 +59,17 @@
     return a * cdf, cdf + a * jnp.exp(-0.5 * a * a) * INV_ROOT2PI
 
 
-def greet(axis, n):
-    me = lax.axis_index(axis)
+def greet(*names_and_sizes):
     barrier = pltpu.get_barrier_semaphore()
-    for step in range(1, n):
-        pl.semaphore_signal(
-            barrier, inc=1, device_id={axis: lax.rem(me + step, n)}, device_id_type=MESH
-        )
-    pl.semaphore_wait(barrier, n - 1)
-    return me
+    count = 0
+    for axis, n in names_and_sizes:
+        me = lax.axis_index(axis)
+        for step in range(1, n):
+            pl.semaphore_signal(
+                barrier, inc=1, device_id={axis: lax.rem(me + step, n)}, device_id_type=MESH
+            )
+            count += 1
+    pl.semaphore_wait(barrier, count)
 
 
 def push(src, dst, send, recv, axis, peer):
@@ -79,13 +81,183 @@
     return copy
 
 
+class WeightGather:
+    def __init__(self, array, n_dp, n_seq):
+        self.array, self.n_dp, self.n_seq = array, n_dp, n_seq
+        self.outs = [jax.ShapeDtypeStruct((n_dp * n_seq,) + array.shape, array.dtype)]
+        sem = pltpu.SemaphoreType.DMA
+        self.scratch = [sem((n_seq,)), sem((n_seq,)), sem((n_dp, n_seq)), sem((n_dp, n_seq)), sem((1,))]
+
+    def across(self, src, block, step):
+        dp = lax.axis_index("dp")
+        return [
+            push(src, self.out.at[block], self.xs.at[k, step], self.xr.at[k, step], "dp",
+                 lax.rem(dp + k, self.n_dp))
+            for k in range(1, self.n_dp)
+        ]
+
+    def begin(self, src, outs, scratch):
+        (self.out,) = outs
+        zs, zr, self.xs, self.xr, local = scratch
+        seq = lax.axis_index("seq")
+        self.base = lax.axis_index("dp") * self.n_seq
+        block = self.base + seq
+        self.along = [
+            push(src, self.out.at[block], zs.at[step], zr.at[step], "seq",
+                 lax.rem(seq + step, self.n_seq))
+            for step in range(1, self.n_seq)
+        ]
+        self.crossing = self.across(src, block, 0)
+        self.own = pltpu.make_async_copy(src, self.out.at[block], local.at[0])
+        self.own.start()
+
+    def end(self):
+        seq = lax.axis_index("seq")
+        for step, copy in enumerate(self.along, 1):
+            copy.wait_recv()
+            block = self.base + lax.rem(seq + self.n_seq - step, self.n_seq)
+            self.crossing += self.across(self.out.at[block], block, step)
+        for copy in self.along:
+            copy.wait_send()
+        for copy in self.crossing:
+            copy.wait()
+        self.own.wait()
+
+
+class GradScatter:
+    def __init__(self, array, n_dp, n_seq):
+        self.array, self.n_dp, self.n_seq = array, n_dp, n_seq
+        shape, kind = array.shape[1:], array.dtype
+        self.outs = [jax.ShapeDtypeStruct(shape, F32)]
+        sem = pltpu.SemaphoreType.DMA
+        self.scratch = [
+            pltpu.VMEM((n_dp - 1, n_seq) + shape, kind),
+            pltpu.VMEM((n_seq,) + shape, kind),
+            pltpu.VMEM((n_seq,) + shape, kind),
+            sem((n_dp, n_seq)), sem((n_dp, n_seq)), sem((n_seq,)), sem((n_seq,)),
+        ]
+
+    def begin(self, src, outs, scratch):
+        self.src, (self.out,) = src, outs
+        self.landx, self.stage, self.landz, xs, xr, self.zs, self.zr = scratch
+        dp, seq = lax.axis_index("dp"), lax.axis_index("seq")
+        self.crossing = {}
+        for step in list(range(1, self.n_seq)) + [0]:
+            to = lax.rem(seq + step, self.n_seq)
+            self.crossing[step] = [
+                push(src.at[lax.rem(dp + k, self.n_dp) * self.n_seq + to],
+                     self.landx.at[k - 1, step], xs.at[k, step], xr.at[k, step], "dp",
+                     lax.rem(dp + k, self.n_dp))
+                for k in range(1, self.n_dp)
+            ]
+
+    def end(self):
+        dp, seq = lax.axis_index("dp"), lax.axis_index("seq")
+        along = []
+        for step in list(range(1, self.n_seq)) + [0]:
+            to = lax.rem(seq + step, self.n_seq)
+            total = self.src[dp * self.n_seq + to].astype(F32)
+            for k, copy in enumerate(self.crossing[step]):
+                copy.wait()
+                total = total + self.landx[k, step].astype(F32)
+            if step:
+                self.stage[step] = total.astype(self.stage.dtype)
+                along.append(
+                    push(self.stage.at[step], self.landz.at[step], self.zs.at[step],
+                         self.zr.at[step], "seq", to))
+        for step, copy in enumerate(along, 1):
+            copy.wait()
+            total = total + self.landz[step].astype(F32)
+        self.out[...] = total
+
+
+class GainSum:
+    def __init__(self, array, n_dp, n_seq, n_ten):
+        self.array, self.sizes = array, (n_ten, n_dp, n_seq)
+        shape = array.shape[1:]
+        self.outs = [jax.ShapeDtypeStruct(shape, F32)]
+        sem = pltpu.SemaphoreType.DMA
+        self.scratch = [
+            pltpu.VMEM((n_ten,) + array.shape, F32),
+            pltpu.VMEM(array.shape, F32),
+            pltpu.VMEM((n_dp, n_seq) + shape, F32),
+            pltpu.VMEM((n_seq,) + shape, F32),
+            pltpu.VMEM((n_seq,) + shape, F32),
+        ] + [sem((n,)) for n in (n_ten, n_ten, n_seq, n_seq)] + [sem((n_dp, n_seq))] * 2
+
+    def begin(self, src, outs, scratch):
+        self.src, (self.out,) = src, outs
+        (self.land, self.total, self.landx, self.stage, self.landz,
+         ys, yr, self.zs, self.zr, self.xs, self.xr) = scratch
+        n_ten = self.sizes[0]
+        me = lax.axis_index("tensor")
+        self.first = [
+            push(src, self.land.at[step], ys.at[step], yr.at[step], "tensor",
+                 lax.rem(me + step, n_ten))
+            for step in range(1, n_ten)
+        ]
+
+    def between(self):
+        _, n_dp, n_seq = self.sizes
+        dp, seq = lax.axis_index("dp"), lax.axis_index("seq")
+        total = self.src[...]
+        for step, copy in enumerate(self.first, 1):
+            copy.wait()
+            total = total + self.land[step]
+        self.total[...] = total
+        self.crossing = {
+            step: [
+                push(self.total.at[lax.rem(dp + k, n_dp) * n_seq + lax.rem(seq + step, n_seq)],
+                     self.landx.at[k, step], self.xs.at[k, step], self.xr.at[k, step], "dp",
+                     lax.rem(dp + k, n_dp))
+                for k in range(1, n_dp)
+            ]
+            for step in range(n_seq)
+        }
+
+    def end(self):
+        _, n_dp, n_seq = self.sizes
+        dp, seq = lax.axis_index("dp"), lax.axis_index("seq")
+        along = []
+        for step in list(range(1, n_seq)) + [0]:
+            to = lax.rem(seq + step, n_seq)
+            total = self.total[dp * n_seq + to]
+            for k, copy in enumerate(self.crossing[step], 1):
+                copy.wait()
+                total = total + self.landx[k, step]
+            if step:
+                self.stage[step] = total
+                along.append(
+                    push(self.stage.at[step], self.landz.at[step], self.zs.at[step],
+                         self.zr.at[step], "seq", to))
+        for step, copy in enumerate(along, 1):
+            copy.wait()
+            total = total + self.landz[step]
+        self.out[...] = total
+
+
+def gather_weights(array, n_dp, n_seq, cid):
+    job = WeightGather(array, n_dp, n_seq)
+
+    def kernel(src, out, *scratch):
+        greet(("dp", n_dp), ("seq", n_seq))
+        job.begin(src, [out], scratch)
+        job.end()
+
+    return pl.pallas_call(
+        kernel, out_shape=job.outs[0], in_specs=[VM], out_specs=VM, scratch_shapes=job.scratch,
+        compiler_params=pltpu.CompilerParams(collective_id=cid, has_side_effects=True),
+    )(array)
+
+
 def gather_blocks(arrays, axis, n, cid):
     count = len(arrays)
 
     def kernel(*refs):
         ins, outs = refs[:count], refs[count : 2 * count]
         send, recv, local = refs[2 * count :]
-        me = greet(axis, n)
+        greet((axis, n))
+        me = lax.axis_index(axis)
         copies = []
         for i in range(count):
             for step in range(1, n):
@@ -118,7 +290,8 @@
     shape = blocks.shape[1:]
 
     def kernel(in_ref, out_ref, land, send, recv):
-        me = greet(axis, n)
+        greet((axis, n))
+        me = lax.axis_index(axis)
         copies = [
             push(in_ref.at[lax.rem(me + step, n)], land.at[step - 1], send.at[step],
                  recv.at[step], axis, lax.rem(me + step, n))
@@ -144,23 +317,28 @@
     )(blocks)
 
 
-def sum_rows_then_gather(partials, extras, middle, gathered, owned, axis, n, cid):
-    np_, ne, ng, no = len(partials), len(extras), len(gathered), len(owned)
+def sum_rows_then_gather(partials, extras, middle, gathered, owned, sizes, jobs, cid):
+    n_dp, n_seq, n = sizes
+    np_, ne, ng, no, nj = len(partials), len(extras), len(gathered), len(owned), len(jobs)
     rows = partials[0].shape[1:]
 
     def kernel(*refs):
         refs = list(refs)
         take = lambda k: [refs.pop(0) for _ in range(k)]
-        parts, more, gouts, oouts, lands = take(np_), take(ne), take(ng), take(no), take(np_)
-        send, recv, gsend, grecv = refs
-        me = greet(axis, n)
+        parts, more, srcs = take(np_), take(ne), take(nj)
+        gouts, oouts, jouts = take(ng), take(no), take(nj)
+        lands, (send, recv, gsend, grecv) = take(np_), take(4)
+        greet(("dp", n_dp), ("seq", n_seq), ("tensor", n))
+        me = lax.axis_index("tensor")
         copies = []
         for i in range(np_):
             copies.append([
                 push(parts[i].at[lax.rem(me + step, n)], lands[i].at[step - 1], send.at[i, step],
-                     recv.at[i, step], axis, lax.rem(me + step, n))
+                     recv.at[i, step], "tensor", lax.rem(me + step, n))
                 for step in range(1, n)
             ])
+        for job, src, out in zip(jobs, srcs, jouts):
+            job.begin(src, [out], take(len(job.scratch)))
         sums = []
         for i in range(np_):
             total = parts[i][me].astype(F32)
@@ -175,28 +353,31 @@
             for step in range(1, n):
                 copies.append(
                     push(gouts[i].at[me], gouts[i].at[me], gsend.at[i, step], grecv.at[i, step],
-                         axis, lax.rem(me + step, n))
+                         "tensor", lax.rem(me + step, n))
                 )
         for i in range(no):
             oouts[i][...] = kept[i].astype(owned[i][1])
+        for job in jobs:
+            if isinstance(job, GainSum):
+                job.between()
+        for job in jobs:
+            job.end()
         for copy in copies:
             copy.wait()
 
+    sem = pltpu.SemaphoreType.DMA
     return pl.pallas_call(
         kernel,
         out_shape=[jax.ShapeDtypeStruct((n,) + s, t) for s, t in gathered]
-        + [jax.ShapeDtypeStruct(s, t) for s, t in owned],
-        in_specs=[VM] * (np_ + ne),
-        out_specs=[VM] * (ng + no),
+        + [jax.ShapeDtypeStruct(s, t) for s, t in owned]
+        + [job.outs[0] for job in jobs],
+        in_specs=[VM] * (np_ + ne + nj),
+        out_specs=[VM] * (ng + no + nj),
         scratch_shapes=[pltpu.VMEM((n - 1,) + rows, p.dtype) for p in partials]
-        + [
-            pltpu.SemaphoreType.DMA((np_, n)),
-            pltpu.SemaphoreType.DMA((np_, n)),
-            pltpu.SemaphoreType.DMA((ng, n)),
-            pltpu.SemaphoreType.DMA((ng, n)),
-        ],
+        + [sem((np_, n)), sem((np_, n)), sem((ng, n)), sem((ng, n))]
+        + [scratch for job in jobs for scratch in job.scratch],
         compiler_params=pltpu.CompilerParams(collective_id=cid, has_side_effects=True),
-    )(*partials, *extras)
+    )(*partials, *extras, *[job.array for job in jobs])
 
 
 def dot(a, b):
@@ -212,7 +393,9 @@
 
 
 def make_per_device(mesh):
-    n_seq, n_ten = mesh.shape["seq"], mesh.shape["tensor"]
+    n_dp, n_seq, n_ten = mesh.shape["dp"], mesh.shape["seq"], mesh.shape["tensor"]
+    sizes = (n_dp, n_seq, n_ten)
+    n_all = n_dp * n_seq
 
     def per_device(tokens, positions, qkv_weight, attn_out_weight, mlp_in_weight, mlp_out_weight,
                    attn_gain, mlp_gain, cotangent):
@@ -222,19 +405,15 @@
         h = w // HD
         wr = qkv_weight.shape[0]
         own = T // n_ten
-        group = ("dp", "seq")
         pack_a = jnp.concatenate(
-            [qkv_weight.reshape(wr, 3 * w), attn_gain[:, None], mlp_gain[:, None]], axis=1)
-        pack_b = jnp.concatenate(
-            [attn_out_weight.T, mlp_in_weight.reshape(wr, 2 * u), mlp_out_weight.T], axis=1)
-        full_a = lax.all_gather(pack_a, group, axis=0, tiled=True)
-        full_b = lax.all_gather(pack_b, group, axis=0, tiled=True)
+            [qkv_weight.reshape(wr, 3 * w), attn_out_weight.T, attn_gain[:, None], mlp_gain[:, None]],
+            axis=1)
+        pack_b = jnp.concatenate([mlp_in_weight.reshape(wr, 2 * u), mlp_out_weight.T], axis=1)
+        full_a = gather_weights(pack_a, n_dp, n_seq, 5).reshape(D, 4 * w + 2)
         w_qkv = full_a[:, : 3 * w]
-        gain1 = full_a[:, 3 * w].astype(F32)[None, :]
-        gain2 = full_a[:, 3 * w + 1].astype(F32)[None, :]
-        w_out_t = full_b[:, :w]
-        w_in = full_b[:, w : w + 2 * u]
-        w_down_t = full_b[:, w + 2 * u :]
+        w_out_t = full_a[:, 3 * w : 4 * w]
+        gain1 = full_a[:, 4 * w].astype(F32)[None, :]
+        gain2 = full_a[:, 4 * w + 1].astype(F32)[None, :]
 
         x = tokens.reshape(T, D)
         cot = cotangent.reshape(T, D)
@@ -279,9 +458,12 @@
             xhat2, _ = layer_norm(mid)
             return [xhat2 * more[1]], [mid]
 
-        normed2, mid_own = sum_rows_then_gather(
+        normed2, mid_own, full_b = sum_rows_then_gather(
             [mid_part], [x_own, gain2], after_attention,
-            [((own, D), BF)], [((own, D), F32)], "tensor", n_ten, 1)
+            [((own, D), BF)], [((own, D), F32)], sizes,
+            [WeightGather(pack_b, n_dp, n_seq)], 1)
+        full_b = full_b.reshape(D, 3 * u)
+        w_in, w_down_t = full_b[:, : 2 * u], full_b[:, 2 * u :]
         normed2 = normed2.reshape(T, D)
         up = dot(normed2, w_in)
         active, slope = gelu_parts(up[:, :u])
@@ -300,20 +482,14 @@
             dmid = dy + norm_backward(dn2 * gain, xhat2, rstd2)
             return [dmid, mid + down], [dmid, gain_grad]
 
-        dmidb, out_rows, dmid_own, g_gain2 = sum_rows_then_gather(
+        g_b = jnp.concatenate([t_dot(normed2, dup).astype(BF), t_dot(dyb, hidden).astype(BF)], axis=1)
+        dmidb, out_rows, dmid_own, g_gain2, sum_b = sum_rows_then_gather(
             [dn2_part, out_part], [mid_own, cot_own, gain2], after_mlp,
             [((own, D), BF), ((own, D), BF)], [((own, D), F32), ((1, D), F32)],
-            "tensor", n_ten, 2)
+            sizes, [GradScatter(g_b.reshape(n_all, wr, 3 * u), n_dp, n_seq)], 2)
         output = out_rows.astype(F32).reshape(S, R, D)
         dmidb = dmidb.reshape(T, D)
         dcontext = dot(dmidb, w_out_t).astype(BF)
-        g_b = jnp.concatenate([
-            t_dot(dmidb, context).astype(BF),
-            t_dot(normed2, dup).astype(BF),
-            t_dot(dyb, hidden).astype(BF),
-        ], axis=1)
-        sum_b = lax.psum_scatter(g_b, group, scatter_dimension=0, tiled=True)
-
         dch = jnp.transpose(dcontext.reshape(S, R, h, HD), (0, 2, 1, 3))
         delta = jnp.sum(dch.astype(F32) * ctx_h.astype(F32), axis=-1, keepdims=True)
         dprobs = jnp.einsum("shqd,shkd->shqk", dch, values, preferred_element_type=F32)
@@ -328,34 +504,33 @@
         dk = unrotate(dkv_own[:, :w].reshape(T, h, HD), cosine, sine)
         dqkv = jnp.concatenate(
             [dq.reshape(T, w), dk.reshape(T, w), dkv_own[:, w:]], axis=1).astype(BF)
-        dn1_part = dot_t(dqkv, w_qkv).astype(BF).reshape(n_ten, own, D)
+        dn1_part = dot_t(dqkv, w_qkv)
+        g_gain1 = jnp.sum(dn1_part * xhat1, axis=0)
+        dn1_part = dn1_part.astype(BF).reshape(n_ten, own, D)
+        gain_grads = jnp.stack([g_gain1, g_gain2[0]]).reshape(2, n_all, wr)
+        gain_grads = jnp.pad(jnp.transpose(gain_grads, (1, 0, 2)), ((0, 0), (0, 6), (0, 128 - wr)))
+        g_a = jnp.concatenate([t_dot(normed1, dqkv).astype(BF), t_dot(dmidb, context).astype(BF)], axis=1)
 
         def at_the_end(sums, more):
-            rows, dmid, gain, gain_grad2 = more
+            rows, dmid, gain = more
             xhat, rstd = layer_norm(rows)
-            dn1 = sums[0]
-            gain_grad1 = jnp.sum(dn1 * xhat, axis=0, keepdims=True)
-            grad = dmid + norm_backward(dn1 * gain, xhat, rstd)
-            pad = jnp.zeros((6, D), F32)
-            return [jnp.concatenate([gain_grad1, gain_grad2, pad], axis=0), grad], []
-
-        gains, grad_rows = sum_rows_then_gather(
-            [dn1_part], [x_own, dmid_own, gain1, g_gain2], at_the_end,
-            [((8, D), F32), ((own, D), BF)], [], "tensor", n_ten, 4)
+            return [dmid + norm_backward(sums[0] * gain, xhat, rstd)], []
+
+        grad_rows, sum_a, gains = sum_rows_then_gather(
+            [dn1_part], [x_own, dmid_own, gain1], at_the_end,
+            [((own, D), BF)], [], sizes,
+            [GradScatter(g_a.reshape(n_all, wr, 4 * w), n_dp, n_seq),
+             GainSum(gain_grads, n_dp, n_seq, n_ten)], 4)
         grad_tokens = grad_rows.astype(F32).reshape(S, R, D)
-        gains = jnp.sum(gains[:, :2], axis=0)
-        g_a = jnp.concatenate([t_dot(normed1, dqkv).astype(BF), gains.T.astype(BF)], axis=1)
-        sum_a = lax.psum_scatter(g_a, group, scatter_dimension=0, tiled=True)
-        sum_a, sum_b = sum_a.astype(F32), sum_b.astype(F32)
         return (
             output,
             grad_tokens,
             sum_a[:, : 3 * w].reshape(wr, 3, w),
-            sum_b[:, :w].T,
-            sum_b[:, w : w + 2 * u].reshape(wr, 2, u),
-            sum_b[:, w + 2 * u :].T,
-            sum_a[:, 3 * w],
-            sum_a[:, 3 * w + 1],
+            sum_a[:, 3 * w :].T,
+            sum_b[:, : 2 * u].reshape(wr, 2, u),
+            sum_b[:, 2 * u :].T,
+            gains[0, :wr],
+            gains[1, :wr],
         )
 
     return per_device

time: 340 us -> 244 us (0.72)
  waiting for transfers between devices: 127 us -> 0 us
  Pallas kernels: 90.9 us -> 163 us
  blocking collectives: 43 us -> 0 us
  between operations: 14.7 us -> 1.38 us
  other arithmetic: 8.47 us -> 15.3 us
  local copies, waits for them, and re-layouts: 37.9 us -> 44.1 us
    unnamed x5 -> x0, waiting for transfers between devices: 127 us -> none
    all_gather x1 -> x0, blocking collectives: 43 us -> none  [per_device(): full_a = lax.all_gather(pack_a, group, axis=0, tiled=True)]
    pallas_call x3, Pallas kernels: 51.4 us -> 91 us  [sum_rows_then_gather(): pl.pallas_call(kernel, out_shape=[jax.ShapeDtypeStruct((n,) + s, t) for s...]
    pallas_call x0 -> x1, Pallas kernels: none -> 29.1 us  [gather_weights(): pl.pallas_call(kernel, out_shape=job.outs[0], in_specs=[VM], out_specs=VM...]
    unnamed x73 -> x54, local copies, waits for them, and re-layouts: 14.3 us -> 9.89 us
  transfers between devices with their start and end apart: 3 -> 0, of which waited for: 2 -> 0; matrix products, arithmetic and copies ran while one was open for 7% -> 0% of each run, Pallas kernels for 6% -> 0%
where the time goes in v2:
time: 244 us; the launch traced here: 243 us
  Pallas kernels  163 us (67%)
  local copies, waits for them, and re-layouts  44.1 us (18%)
  matrix products  19.3 us (8%)
  other arithmetic  15.3 us (6%)
    pallas_call x3, Pallas kernels, sum_rows_then_gather(): pl.pallas_call(kernel, out_shape=[jax.ShapeDtypeStruct((n,) + s, t) for s...  91 us
    pallas_call x1, Pallas kernels, gather_weights(): pl.pallas_call(kernel, out_shape=job.outs[0], in_specs=[VM], out_specs=VM...  29.1 us
    pallas_call x1, Pallas kernels, gather_blocks(): pl.pallas_call(kernel, out_shape=[jax.ShapeDtypeStruct((n,) + a.shape, a....  23.4 us
    pallas_call x1, Pallas kernels, scatter_sum(): pl.pallas_call(kernel, out_shape=jax.ShapeDtypeStruct(shape, F32), in_spe...  19.5 us
    unnamed x54, local copies, waits for them, and re-layouts  9.89 us
    dot_general x4, matrix products, dot(): return jnp.dot(a, b, preferred_element_type=F32)  7.29 us
    dot_general x4, matrix products, dot_t(): lax.dot_general(a, b, (((1,), (1,)), ((), ())), preferred_element_type=F32)  6.06 us

profile of v2, /device:TPU:0, one launch (start us, length us, event | category | flops | bytes accessed | tf_op | source)
XLA Modules:
  0.0 243.0 jit_solution(16884608421747023380)
XLA Ops:
  2.2 0.9 copy.83
  3.1 1.1 copy.82
  5.1 29.1 %shard_map.152 = bf16[8,96,770]{2,1,0:T(8,128)(2,1)} custom-call(bf16[96,770]{1,0:T(8,128)(2,1)} %pad_maximum_fusion.9.src), custom_call_target="tpu_custom_call" | custom-call | tf_op jit(solution)/shard_map/pallas_call | solution.py:247
  34.2 1.8 fusion.42
  36.5 0.9 multiply_convert_fusion.2
  38.2 1.4 fusion.49
  42.9 23.4 %shard_map.153 = (bf16[4,256,384]{2,1,0:T(8,128)(2,1)}, s32[4,8,128]{2,1,0:T(8,128)}) custom-call(bf16[256,384]{1,0:T(8,128)(2,1)} %pad_maximum_fusion.4.refs_0_, s32[8,128]{1,0:T(8,128)} %pad.8.refs_1_), custom_call_target="tpu_custom_call" | custom-call | tf_op jit(solution)/shard_map/pallas_call | solution.py:275
  66.4 1.4 copy.95
  68.0 0.8 fusion.43
  69.1 0.9 squeeze.30
  74.1 1.2 convolution_convert_fusion.6
  75.3 1.8 constant_dynamic-slice_fusion
  77.1 1.0 copy.120
  78.8 1.6 copy.100
  80.4 1.7 reshape.284
  82.1 1.7 pad_maximum_fusion.10.refs_3_
  83.8 26.4 %shard_map.154 = (bf16[4,64,768]{2,1,0:T(8,128)(2,1)}, f32[64,768]{1,0:T(8,128)}, bf16[8,96,864]{2,1,0:T(8,128)(2,1)}) custom-call(bf16[4,64,768]{2,1,0:T(8,128)(2,1)} %bitcast.175, f32[64,768]{1,0:T(8,128)} %get-tuple-element.104.refs_1_, f32[1,768]{1,0:T(1,128)} %bitcast_convert_fusion.2.refs_2_.refs_4_, bf16[96,864]{1,0:T(8,128)(2,1)} %pad_maximum_fusion.10.refs_3_), custom_call_target="tpu_custom_call" | custom-call | tf_op jit(solution)/shard_map/pallas_call | solution.py:369
  110.2 1.9 fusion.3
  112.1 1.8 fusion.19
  113.9 1.3 convolution_convert_fusion.5
  115.2 1.3 convolution_convert_fusion.7
  117.3 1.2 pad_maximum_fusion
  118.4 2.5 %copy.101 = bf16[768,864]{1,0:T(8,128)(2,1)} copy(bf16[768,864]{0,1:T(8,128)(2,1)} %pad_maximum_fusion) | data formatting | bytes 2654208 | tf_op jit(solution)/shard_map/concatenate | solution.py:485
  120.9 30.2 %shard_map.155 = (bf16[4,64,768]{2,1,0:T(8,128)(2,1)}, bf16[4,64,768]{2,1,0:T(8,128)(2,1)}, f32[64,768]{1,0:T(8,128)}, f32[1,768]{1,0:T(1,128)}, f32[96,864]{1,0:T(8,128)}) custom-call(bf16[4,64,768]{2,1,0:T(8,128)(2,1)} %bitcast.198, bf16[4,64,768]{2,1,0:T(8,128)(2,1)} %bitcast.177, f32[64,768]{1,0:T(8,128)} %get-tuple-element.25.refs_2_, ...), custom_call_target="tpu_custom_call" | custom-call | tf_op jit(solution)/shard_map/pallas_call | solution.py:369
  151.2 1.9 bitcast_convert_fusion.1
  153.1 2.2 convolution_convert_fusion.10
  155.3 0.9 reshape.294
  156.2 1.2 convolution_convert_fusion.3
  157.4 1.8 stack.18
  159.2 2.2 copy.108
  161.4 1.0 multiply_reduce_fusion.2
  162.4 1.5 multiply_convert_fusion
  163.9 0.9 copy-done.3
  165.8 1.1 maximum_bitcast_fusion
  167.4 1.2 copy.109.in_ref
  168.6 19.5 %shard_map.156 = f32[256,384]{1,0:T(8,128)} custom-call(bf16[4,256,384]{2,1,0:T(8,128)(2,1)} %copy.109.in_ref), custom_call_target="tpu_custom_call" | custom-call | tf_op jit(solution)/shard_map/pallas_call | solution.py:306
  188.1 1.7 slice.193
  189.8 1.0 slice.114
  191.3 0.9 bitcast_multiply_fusion.1
  193.8 2.2 multiply_reduce_fusion
  197.6 1.5 copy.113
  199.9 34.3 %shard_map.157 = (bf16[4,64,768]{2,1,0:T(8,128)(2,1)}, f32[96,768]{1,0:T(8,128)}, f32[8,128]{1,0:T(8,128)}) custom-call(bf16[4,64,768]{2,1,0:T(8,128)(2,1)} %bitcast.195, f32[64,768]{1,0:T(8,128)} %get-tuple-element.104.refs_1_, f32[64,768]{1,0:T(8,128)} %get-tuple-element.28.refs_2_, f32[1,768]{1,0:T(1,128)} %convert_bitcast_fusion.refs_3_, ...), custom_call_target="tpu_custom_call" | custom-call | tf_op jit(solution)/shard_map/pallas_call | solution.py:369
  234.2 2.0 bitcast_convert_fusion
  236.2 1.0 slice.118
  237.3 0.9 copy.115
  238.2 1.0 slice_bitcast_fusion.3
  239.9 0.9 reshape.304
  241.8 1.3 slice_bitcast_fusion.5
  (126 shorter events, 20.2 us)
Async XLA Ops:
  4.1 32.0 %copy-start.1 = (f32[2,128,768]{2,1,0:T(8,128)S(1)}, f32[2,128,768]{2,1,0:T(8,128)}, u32[]{:S(2)}) copy-start(f32[2,128,768]{2,1,0:T(8,128)} %param.9) | copy-start | bytes 2359300
  36.0 1.5 copy-start
  38.2 2.3 copy-start.22
  40.7 0.6 copy-start.18
  68.0 2.0 copy-start.17
  70.4 1.9 copy-start.12
  71.8 1.1 copy-start.5
  73.4 36.8 %copy-start.14 = (bf16[2,3,128,64]{2,3,1,0:T(8,128)(2,1)}, bf16[2,3,128,64]{2,3,1,0:T(8,128)(2,1)S(1)}, u32[]{:S(2)}) copy-start(bf16[2,3,128,64]{2,3,1,0:T(8,128)(2,1)S(1)} %convolution_convert_fusion.9) | copy-start | bytes 294916
  73.5 0.6 copy-start.15
  110.2 1.9 copy-start.7
  113.9 2.6 %copy-start.11 = (f32[2,128,768]{2,1,0:T(8,128)S(1)}, f32[2,128,768]{2,1,0:T(8,128)}, u32[]{:S(2)}) copy-start(f32[2,128,768]{2,1,0:T(8,128)} %param.17) | copy-start | bytes 2359300
  115.2 1.6 copy-start.10
  161.4 3.4 %copy-start.13 = (bf16[2,3,128,64]{2,3,1,0:T(8,128)(2,1)S(1)}, bf16[2,3,128,64]{2,3,1,0:T(8,128)(2,1)}, u32[]{:S(2)}) copy-start(bf16[2,3,128,64]{2,3,1,0:T(8,128)(2,1)} %copy-done.12) | copy-start | bytes 294916
  163.9 0.9 copy-start.3
  164.8 1.0 copy-start.9
  168.6 22.3 %copy-start.4 = (bf16[2,3,128,512]{3,2,1,0:T(8,128)(2,1)S(1)}, bf16[2,3,128,512]{3,2,1,0:T(8,128)(2,1)}, u32[]{:S(2)}) copy-start(bf16[2,3,128,512]{3,2,1,0:T(8,128)(2,1)} %copy-done.3) | copy-start | bytes 2359300
  191.3 1.3 copy-start.6
  192.6 1.1 copy-start.2
  193.8 2.8 %copy-start.8 = (bf16[4,64,768]{2,1,0:T(8,128)(2,1)S(1)}, bf16[4,64,768]{2,1,0:T(8,128)(2,1)}, u32[]{:S(2)}) copy-start(bf16[4,64,768]{2,1,0:T(8,128)(2,1)} %get-tuple-element.27) | copy-start | bytes 1179652
  193.8 2.8 %copy-start.16 = (bf16[2,128,3,64]{1,0,3,2:T(2,128)(2,1)S(1)}, bf16[2,128,3,64]{1,0,3,2:T(2,128)(2,1)}, u32[]{:S(2)}) copy-start(bf16[2,128,3,64]{1,0,3,2:T(2,128)(2,1)} %copy-done.15) | copy-start | bytes 294916
  193.8 3.1 %copy-start.20 = (bf16[256,192]{1,0:T(8,128)(2,1)S(1)}, bf16[256,192]{1,0:T(8,128)(2,1)}, u32[]{:S(2)}) copy-start(bf16[256,192]{1,0:T(8,128)(2,1)} %slice.193) | copy-start | bytes 294916
  197.6 1.5 copy-start.21
  234.2 5.7 %copy-start.19 = (f32[96,864]{1,0:T(8,128)S(1)}, f32[96,864]{1,0:T(8,128)}, u32[]{:S(2)}) copy-start(f32[96,864]{1,0:T(8,128)} %get-tuple-element.32) | copy-start | bytes 995332

commit v3 on v2

--- a/solution.py
+++ b/solution.py
@@ -248,42 +248,6 @@
         kernel, out_shape=job.outs[0], in_specs=[VM], out_specs=VM, scratch_shapes=job.scratch,
         compiler_params=pltpu.CompilerParams(collective_id=cid, has_side_effects=True),
     )(array)
-
-
-def gather_blocks(arrays, axis, n, cid):
-    count = len(arrays)
-
-    def kernel(*refs):
-        ins, outs = refs[:count], refs[count : 2 * count]
-        send, recv, local = refs[2 * count :]
-        greet((axis, n))
-        me = lax.axis_index(axis)
-        copies = []
-        for i in range(count):
-            for step in range(1, n):
-                copies.append(
-                    push(ins[i], outs[i].at[me], send.at[i, step], recv.at[i, step], axis,
-                         lax.rem(me + step, n))
-                )
-        for i in range(count):
-            own = pltpu.make_async_copy(ins[i], outs[i].at[me], local.at[i])
-            own.start()
-            own.wait()
-        for copy in copies:
-            copy.wait()
-
-    return pl.pallas_call(
-        kernel,
-        out_shape=[jax.ShapeDtypeStruct((n,) + a.shape, a.dtype) for a in arrays],
-        in_specs=[VM] * count,
-        out_specs=[VM] * count,
-        scratch_shapes=[
-            pltpu.SemaphoreType.DMA((count, n)),
-            pltpu.SemaphoreType.DMA((count, n)),
-            pltpu.SemaphoreType.DMA((count,)),
-        ],
-        compiler_params=pltpu.CompilerParams(collective_id=cid, has_side_effects=True),
-    )(*arrays)
 
 
 def scatter_sum(blocks, axis, n, cid):
@@ -392,6 +356,89 @@
     return lax.dot_general(a, b, (((0,), (0,)), ((), ())), preferred_element_type=F32)
 
 
+def attention_stage(kv, starts8, q, q_start, w_out_t, x_own, gain, pack_b, sizes, S, cid):
+    n_dp, n_seq, n = sizes
+    T, w = q.shape
+    R, h, own = T // S, w // HD, x_own.shape[0]
+    L = R * n_seq
+    scale = 1.0 / math.sqrt(HD)
+    job = WeightGather(pack_b, n_dp, n_seq)
+
+    def kernel(kv_ref, st_ref, q_ref, qs_ref, wo_ref, x_ref, gain_ref, pb_ref,
+               normed_out, mid_out, ctx_out, lse_out, kv_all, st_all, pb_out,
+               part, land, ksend, krecv, local, send, recv, gsend, grecv, *rest):
+        greet(("dp", n_dp), ("seq", n_seq), ("tensor", n))
+        me, seq = lax.axis_index("tensor"), lax.axis_index("seq")
+        arriving = []
+        for i, (src, dst) in enumerate(((st_ref, st_all), (kv_ref, kv_all))):
+            for step in range(1, n_seq):
+                arriving.append(
+                    push(src, dst.at[seq], ksend.at[i, step], krecv.at[i, step], "seq",
+                         lax.rem(seq + step, n_seq)))
+            mine = pltpu.make_async_copy(src, dst.at[seq], local.at[i])
+            mine.start()
+            mine.wait()
+        job.begin(pb_ref, [pb_out], rest)
+        for copy in arriving:
+            copy.wait()
+        for s in range(S):
+            rows = slice(s * R, (s + 1) * R)
+            k_start = jnp.concatenate([st_all[j, s : s + 1, :] for j in range(n_seq)], axis=1)
+            same = qs_ref[rows, :] == k_start
+            heads = []
+            for i in range(h):
+                cols = slice(i * HD, (i + 1) * HD)
+                keys = kv_all[:, rows, cols].reshape(L, HD)
+                values = kv_all[:, rows, w + i * HD : w + (i + 1) * HD].reshape(L, HD)
+                scores = jnp.where(same, dot_t(q_ref[rows, cols], keys) * scale, -jnp.inf)
+                top = jnp.max(scores, axis=-1, keepdims=True)
+                lse = top + jnp.log(jnp.sum(jnp.exp(scores - top), axis=-1, keepdims=True))
+                lse_out[s * h + i] = lse
+                probs = jnp.exp(scores - lse).astype(BF)
+                heads.append(dot(probs, values).astype(BF))
+            ctx_out[rows, :] = jnp.concatenate(heads, axis=1)
+        projected = dot_t(ctx_out[...], wo_ref[...]).astype(BF)
+        for i in range(n):
+            part[i] = projected[i * own : (i + 1) * own]
+        copies = [
+            push(part.at[lax.rem(me + step, n)], land.at[step - 1], send.at[step], recv.at[step],
+                 "tensor", lax.rem(me + step, n))
+            for step in range(1, n)
+        ]
+        total = part[me].astype(F32)
+        for step, copy in enumerate(copies):
+            copy.wait()
+            total = total + land[step].astype(F32)
+        mid = x_ref[...] + total
+        mid_out[...] = mid
+        xhat, _ = layer_norm(mid)
+        normed_out[me] = (xhat * gain_ref[...]).astype(BF)
+        copies = [
+            push(normed_out.at[me], normed_out.at[me], gsend.at[step], grecv.at[step],
+                 "tensor", lax.rem(me + step, n))
+            for step in range(1, n)
+        ]
+        job.end()
+        for copy in copies:
+            copy.wait()
+
+    sem = pltpu.SemaphoreType.DMA
+    struct = jax.ShapeDtypeStruct
+    args = (kv, starts8, q, q_start, w_out_t, x_own, gain, pack_b)
+    outs = [
+        struct((n, own, D), BF), struct((own, D), F32), struct((T, w), BF),
+        struct((S * h, R, 1), F32), struct((n_seq,) + kv.shape, BF),
+        struct((n_seq,) + starts8.shape, jnp.int32)] + job.outs
+    return pl.pallas_call(
+        kernel, out_shape=outs, in_specs=[VM] * len(args), out_specs=[VM] * len(outs),
+        scratch_shapes=[
+            pltpu.VMEM((n, own, D), BF), pltpu.VMEM((n - 1, own, D), BF),
+            sem((2, n_seq)), sem((2, n_seq)), sem((2,)), sem((n,)), sem((n,)), sem((n,)), sem((n,)),
+        ] + job.scratch,
+        compiler_params=pltpu.CompilerParams(collective_id=cid, has_side_effects=True),
+    )(*args)
+
+
 def make_per_device(mesh):
     n_dp, n_seq, n_ten = mesh.shape["dp"], mesh.shape["seq"], mesh.shape["tensor"]
     sizes = (n_dp, n_seq, n_ten)
@@ -434,34 +481,9 @@
         v = qkv[:, 2].astype(BF)
         kv = jnp.concatenate([k.reshape(T, w), v.reshape(T, w)], axis=1)
         starts8 = jnp.pad(starts, ((0, 8 - S), (0, 0)))
-        kv_all, starts_all = gather_blocks([kv, starts8], "seq", n_seq, 0)
-        k_start = jnp.transpose(starts_all[:, :S], (1, 0, 2)).reshape(S, L)
-        kv_heads = jnp.transpose(
-            kv_all.reshape(n_seq, S, R, 2, h, HD), (3, 1, 4, 0, 2, 5)).reshape(2, S, h, L, HD)
-        keys, values = kv_heads[0], kv_heads[1]
-        qh = jnp.transpose(q.reshape(S, R, h, HD), (0, 2, 1, 3))
-        scale = 1.0 / math.sqrt(HD)
-        mask = (starts[:, :, None] == k_start[:, None, :])[:, None]
-        scores = jnp.einsum("shqd,shkd->shqk", qh, keys, preferred_element_type=F32) * scale
-        scores = jnp.where(mask, scores, -jnp.inf)
-        top = jnp.max(scores, axis=-1, keepdims=True)
-        lse = top + jnp.log(jnp.sum(jnp.exp(scores - top), axis=-1, keepdims=True))
-        probs32 = jnp.exp(scores - lse)
-        probs = probs32.astype(BF)
-        ctx_h = jnp.einsum("shqk,shkd->shqd", probs, values, preferred_element_type=F32).astype(BF)
-        context = jnp.transpose(ctx_h, (0, 2, 1, 3)).reshape(T, w)
-
-        mid_part = dot_t(context, w_out_t).astype(BF).reshape(n_ten, own, D)
-
-        def after_attention(sums, more):
-            mid = more[0] + sums[0]
-            xhat2, _ = layer_norm(mid)
-            return [xhat2 * more[1]], [mid]
-
-        normed2, mid_own, full_b = sum_rows_then_gather(
-            [mid_part], [x_own, gain2], after_attention,
-            [((own, D), BF)], [((own, D), F32)], sizes,
-            [WeightGather(pack_b, n_dp, n_seq)], 1)
+        q_start = starts.reshape(T, 1)
+        normed2, mid_own, context, lse, kv_all, starts_all, full_b = attention_stage(
+            kv, starts8, q.reshape(T, w), q_start, w_out_t, x_own, gain2, pack_b, sizes, S, 1)
         full_b = full_b.reshape(D, 3 * u)
         w_in, w_down_t = full_b[:, : 2 * u], full_b[:, 2 * u :]
         normed2 = normed2.reshape(T, D)
@@ -490,6 +512,18 @@
         output = out_rows.astype(F32).reshape(S, R, D)
         dmidb = dmidb.reshape(T, D)
         dcontext = dot(dmidb, w_out_t).astype(BF)
+        k_start = jnp.transpose(starts_all[:, :S], (1, 0, 2)).reshape(S, L)
+        kv_heads = jnp.transpose(
+            kv_all.reshape(n_seq, S, R, 2, h, HD), (3, 1, 4, 0, 2, 5)).reshape(2, S, h, L, HD)
+        keys, values = kv_heads[0], kv_heads[1]
+        qh = jnp.transpose(q.reshape(S, R, h, HD), (0, 2, 1, 3))
+        ctx_h = jnp.transpose(context.reshape(S, R, h, HD), (0, 2, 1, 3))
+        scale = 1.0 / math.sqrt(HD)
+        mask = (starts[:, :, None] == k_start[:, None, :])[:, None]
+        scores = jnp.einsum("shqd,shkd->shqk", qh, keys, preferred_element_type=F32) * scale
+        scores = jnp.where(mask, scores, -jnp.inf)
+        probs32 = jnp.exp(scores - lse.reshape(S, h, R, 1))
+        probs = probs32.astype(BF)
         dch = jnp.transpose(dcontext.reshape(S, R, h, HD), (0, 2, 1, 3))
         delta = jnp.sum(dch.astype(F32) * ctx_h.astype(F32), axis=-1, keepdims=True)
         dprobs = jnp.einsum("shqd,shkd->shqk", dch, values, preferred_element_type=F32)

time: 244 us -> 258 us (1.057)
  other arithmetic: 15.3 us -> 24.3 us
  Pallas kernels: 163 us -> 169 us
    pallas_call x1, Pallas kernels: 23.4 us -> 47.9 us  [attention_stage(): pl.pallas_call(kernel, out_shape=outs, in_specs=[VM] * len(args), out_spe...]
    pallas_call x3 -> x2, Pallas kernels: 91 us -> 70.8 us  [sum_rows_then_gather(): pl.pallas_call(kernel, out_shape=[jax.ShapeDtypeStruct((n,) + s, t) for s...]
    unnamed x54 -> x72, local copies, waits for them, and re-layouts: 9.89 us -> 2.9 us
    convert_element_type x1 -> x4, local copies, waits for them, and re-layouts: 0.1 us -> 4.57 us  [the longest x2 3.39 us: per_device(): delta = jnp.sum(dch.astype(F32) * ctx_h.astype(F32), axis=-1, keepdims=True)]
    mul x4 -> x6, local copies, waits for them, and re-layouts: 0.4 us -> 3.22 us  [rotate(): return values * cosine[:, None, :] + turned * sine[:, None, :]]
    dot_general x4 -> x3, matrix products: 6.06 us -> 4.83 us  [dot_t(): lax.dot_general(a, b, (((1,), (1,)), ((), ())), preferred_element_type=F32)]
where the time goes in v3:
time: 258 us; the launch traced here: 257 us
  Pallas kernels  169 us (66%)
  local copies, waits for them, and re-layouts  45.1 us (17%)
  other arithmetic  24.3 us (9%)
  matrix products  17.4 us (7%)
    pallas_call x2, Pallas kernels, sum_rows_then_gather(): pl.pallas_call(kernel, out_shape=[jax.ShapeDtypeStruct((n,) + s, t) for s...  70.8 us
    pallas_call x1, Pallas kernels, attention_stage(): pl.pallas_call(kernel, out_shape=outs, in_specs=[VM] * len(args), out_spe...  47.9 us
    pallas_call x1, Pallas kernels, gather_weights(): pl.pallas_call(kernel, out_shape=job.outs[0], in_specs=[VM], out_specs=VM...  29.1 us
    pallas_call x1, Pallas kernels, scatter_sum(): pl.pallas_call(kernel, out_shape=jax.ShapeDtypeStruct(shape, F32), in_spe...  21.2 us
    dot_general x4, matrix products, dot(): return jnp.dot(a, b, preferred_element_type=F32)  5.68 us

profile of v3, /device:TPU:0, one launch (start us, length us, event | category | flops | bytes accessed | tf_op | source)
XLA Modules:
  0.0 257.3 jit_solution(16227144459493676309)
XLA Ops:
  0.7 1.4 reduce_sum.36
  2.7 1.4 multiply_reduce_fusion.1
  11.1 1.7 constant_dynamic-slice_fusion
  12.8 29.1 %shard_map.152 = bf16[8,96,770]{2,1,0:T(8,128)(2,1)} custom-call(bf16[96,770]{1,0:T(8,128)(2,1)} %pad_maximum_fusion.9.src), custom_call_target="tpu_custom_call" | custom-call | tf_op jit(solution)/shard_map/pallas_call | solution.py:247
  41.9 1.4 convert_reduce_fusion
  44.7 0.9 slice.133.wo_ref
  45.7 1.3 copy.136
  47.0 1.6 fusion.38
  49.7 1.6 bitcast_multiply_fusion.1
  51.3 1.1 copy.140
  52.4 1.7 slice_negate_fusion.3
  54.9 1.1 copy.141
  56.7 0.9 copy.188
  57.6 0.9 copy.189
  58.5 1.5 fusion.23
  61.0 47.9 %shard_map.153 = (bf16[4,64,768]{2,1,0:T(8,128)(2,1)}, f32[64,768]{1,0:T(8,128)}, bf16[256,192]{1,0:T(8,128)(2,1)}, f32[6,128,1]{2,1,0:T(8,128)}, bf16[4,256,384...) custom-call(bf16[256,384]{1,0:T(8,128)(2,1)} %pad_maximum_fusion.4.kv_ref, s32[8,128]{1,0:T(8,128)} %pad.8.st_ref, ...), custom_call_target="tpu_custom_call" | custom-call | tf_op jit(solution)/shard_map/pallas_call | solution.py:432
  109.7 1.3 reduce.4
  112.3 1.7 copy.152
  114.0 1.7 reshape.310
  115.7 1.9 fusion.2
  118.3 1.3 convolution_convert_fusion.5
  119.6 1.3 convolution_convert_fusion.6
  121.7 1.6 copy.144
  123.3 36.3 %shard_map.154 = (bf16[4,64,768]{2,1,0:T(8,128)(2,1)}, bf16[4,64,768]{2,1,0:T(8,128)(2,1)}, f32[64,768]{1,0:T(8,128)}, f32[1,768]{1,0:T(1,128)}, f32[96,864]{1,0:T(8,128)}) custom-call(bf16[4,64,768]{2,1,0:T(8,128)(2,1)} %bitcast.192, bf16[4,64,768]{2,1,0:T(8,128)(2,1)} %bitcast.171, f32[64,768]{1,0:T(8,128)} %get-tuple-element.25.refs_2_, ...), custom_call_target="tpu_custom_call" | custom-call | tf_op jit(solution)/shard_map/pallas_call | solution.py:333
  160.4 1.5 convolution_convert_fusion.8
  162.0 2.0 convolution_convert_fusion.7
  165.1 0.9 reshape.302
  166.0 0.9 bitcast_convert_fusion.1
  167.0 2.3 copy.148
  169.2 2.2 reshape.290
  172.6 0.9 squeeze.33
  174.0 1.5 subtract_exponential_fusion
  175.9 1.0 convolution_convert_fusion.3
  178.1 1.1 stack.18
  179.6 1.1 maximum_bitcast_fusion
  180.7 1.4 reshape.295
  182.1 2.3 copy.161.in_ref
  184.4 21.2 %shard_map.155 = f32[256,384]{1,0:T(8,128)} custom-call(bf16[4,256,384]{2,1,0:T(8,128)(2,1)} %copy.161.in_ref), custom_call_target="tpu_custom_call" | custom-call | tf_op jit(solution)/shard_map/pallas_call | solution.py:270
  205.7 1.8 slice.193
  209.3 1.1 copy.157
  210.4 1.0 fusion.36
  211.7 2.2 multiply_reduce_fusion
  215.3 1.5 copy.165
  216.8 34.5 %shard_map.156 = (bf16[4,64,768]{2,1,0:T(8,128)(2,1)}, f32[96,768]{1,0:T(8,128)}, f32[8,128]{1,0:T(8,128)}) custom-call(bf16[4,64,768]{2,1,0:T(8,128)(2,1)} %bitcast.190, f32[64,768]{1,0:T(8,128)} %get-tuple-element.122.x_ref.refs_1_, f32[64,768]{1,0:T(8,128)} %get-tuple-element.32.refs_2_, f32[1,768]{1,0:T(1,128)} %reshape.307.refs_3_, ...), custom_call_target="tpu_custom_call" | custom-call | tf_op jit(solution)/shard_map/pallas_call | solution.py:333
  251.4 1.3 slice_bitcast_fusion.4
  252.6 1.0 slice_bitcast_fusion.2
  253.6 1.0 slice.118
  256.4 0.9 bitcast_convert_fusion
  (148 shorter events, 26.8 us)
Async XLA Ops:
  0.6 4.7 %copy-start.32 = (bf16[96]{0:T(256)(128)(2,1)S(1)}, bf16[96]{0:T(256)(128)(2,1)}, u32[]{:S(2)}) copy-start(bf16[96]{0:T(256)(128)(2,1)} %param.16) | copy-start | bytes 580
  0.6 4.6 %copy-start.31 = (bf16[96]{0:T(256)(128)(2,1)S(1)}, bf16[96]{0:T(256)(128)(2,1)}, u32[]{:S(2)}) copy-start(bf16[96]{0:T(256)(128)(2,1)} %param.15) | copy-start | bytes 580
  0.7 6.7 %copy-start.24 = (bf16[288,96]{1,0:T(8,128)(2,1)S(1)}, bf16[288,96]{1,0:T(8,128)(2,1)}, u32[]{:S(2)}) copy-start(bf16[288,96]{1,0:T(8,128)(2,1)} %param.14) | copy-start | bytes 165892
  0.7 6.8 %copy-start.21 = (bf16[96,2,288]{2,1,0:T(2,128)(2,1)S(1)}, bf16[96,2,288]{2,1,0:T(2,128)(2,1)}, u32[]{:S(2)}) copy-start(bf16[96,2,288]{2,1,0:T(2,128)(2,1)} %param.13) | copy-start | bytes 331780
  0.7 4.8 %copy-start.25 = (bf16[192,96]{1,0:T(8,128)(2,1)S(1)}, bf16[192,96]{1,0:T(8,128)(2,1)}, u32[]{:S(2)}) copy-start(bf16[192,96]{1,0:T(8,128)(2,1)} %param.12) | copy-start | bytes 110596
  0.7 4.0 %copy-start.30 = (s32[2,128]{1,0:T(2,128)S(1)}, s32[2,128]{1,0:T(2,128)}, u32[]{:S(2)}) copy-start(s32[2,128]{1,0:T(2,128)} %param.10) | copy-start | bytes 3076
  0.7 8.4 %copy-start.22 = (bf16[96,3,192]{2,0,1:T(8,128)(2,1)S(1)}, bf16[96,3,192]{2,0,1:T(8,128)(2,1)}, u32[]{:S(2)}) copy-start(bf16[96,3,192]{2,0,1:T(8,128)(2,1)} %param.11) | copy-start | bytes 331780
  5.6 5.5 %copy-start.1 = (f32[2,128,768]{2,1,0:T(8,128)S(1)}, f32[2,128,768]{2,1,0:T(8,128)}, u32[]{:S(2)}) copy-start(f32[2,128,768]{2,1,0:T(8,128)} %param.9) | copy-start | bytes 2359300
  6.7 6.1 %copy-start.9 = (f32[256,64]{0,1:T(8,128)}, f32[256,64]{0,1:T(8,128)S(1)}, u32[]{:S(2)}) copy-start(f32[256,64]{0,1:T(8,128)S(1)} %get-tuple-element.119) | copy-start | bytes 196612
  41.9 2.8 %copy-start = (bf16[8,96,770]{2,1,0:T(8,128)(2,1)S(1)}, bf16[8,96,770]{2,1,0:T(8,128)(2,1)}, u32[]{:S(2)}) copy-start(bf16[8,96,770]{2,1,0:T(8,128)(2,1)} %shard_map.152) | copy-start | bytes 3548164
  47.0 2.7 %copy-start.10 = (f32[256,64]{0,1:T(8,128)S(1)}, f32[256,64]{0,1:T(8,128)}, u32[]{:S(2)}) copy-start(f32[256,64]{0,1:T(8,128)} %copy-done.9) | copy-start | bytes 196612
  49.6 2.8 %copy-start.13 = (f32[256,3,64]{0,2,1:T(8,128)S(1)}, f32[256,3,64]{0,2,1:T(8,128)}, u32[]{:S(2)}) copy-start(f32[256,3,64]{0,2,1:T(8,128)} %get-tuple-element.79) | copy-start | bytes 589828
  49.6 4.5 %copy-start.14 = (f32[256,64]{0,1:T(8,128)S(1)}, f32[256,64]{0,1:T(8,128)}, u32[]{:S(2)}) copy-start(f32[256,64]{0,1:T(8,128)} %get-tuple-element.120) | copy-start | bytes 196612
  109.7 8.0 %copy-start.3 = (bf16[8,96,864]{2,1,0:T(8,128)(2,1)S(1)}, bf16[8,96,864]{2,1,0:T(8,128)(2,1)}, u32[]{:S(2)}) copy-start(bf16[8,96,864]{2,1,0:T(8,128)(2,1)} %get-tuple-element.23) | copy-start | bytes 3981316
  115.7 1.9 copy-start.6
  118.3 2.6 %copy-start.5 = (bf16[4,64,768]{2,1,0:T(8,128)(2,1)S(1)}, bf16[4,64,768]{2,1,0:T(8,128)(2,1)}, u32[]{:S(2)}) copy-start(bf16[4,64,768]{2,1,0:T(8,128)(2,1)} %get-tuple-element.24) | copy-start | bytes 1179652
  123.3 38.7 %copy-start.16 = (bf16[256,192]{1,0:T(8,128)(2,1)S(1)}, bf16[256,192]{1,0:T(8,128)(2,1)}, u32[]{:S(2)}) copy-start(bf16[256,192]{1,0:T(8,128)(2,1)} %get-tuple-element.31) | copy-start | bytes 294916
  159.6 4.5 %copy-start.12 = (f32[2,128,3,64]{1,0,3,2:T(2,128)S(1)}, f32[2,128,3,64]{1,0,3,2:T(2,128)}, u32[]{:S(2)}) copy-start(f32[2,128,3,64]{1,0,3,2:T(2,128)} %reshape.310) | copy-start | bytes 589828
  159.6 4.6 %copy-start.17 = (f32[96,864]{1,0:T(8,128)S(1)}, f32[96,864]{1,0:T(8,128)}, u32[]{:S(2)}) copy-start(f32[96,864]{1,0:T(8,128)} %get-tuple-element.36) | copy-start | bytes 995332
  162.0 4.1 %copy-start.19 = (bf16[4,64,768]{2,1,0:T(8,128)(2,1)S(1)}, bf16[4,64,768]{2,1,0:T(8,128)(2,1)}, u32[]{:S(2)}) copy-start(bf16[4,64,768]{2,1,0:T(8,128)(2,1)} %get-tuple-element.26) | copy-start | bytes 1179652
  172.3 1.7 copy-start.18
  172.3 1.7 copy-start.26
  173.8 1.7 copy-start.4
  182.1 25.5 %copy-start.11 = (f32[256,64]{0,1:T(8,128)S(1)}, f32[256,64]{0,1:T(8,128)}, u32[]{:S(2)}) copy-start(f32[256,64]{0,1:T(8,128)} %copy-done.9) | copy-start | bytes 196612
  205.6 2.1 slice-start
  205.6 2.2 copy-start.15
  208.6 3.0 %copy-start.2 = (f32[256,384]{1,0:T(8,128)S(1)}, f32[256,384]{1,0:T(8,128)}, u32[]{:S(2)}) copy-start(f32[256,384]{1,0:T(8,128)} %shard_map.155) | copy-start | bytes 1179652
  208.6 3.0 %copy-start.8 = (f32[256,192]{1,0:T(8,128)S(1)}, f32[256,192]{1,0:T(8,128)}, u32[]{:S(2)}) copy-start(f32[256,192]{1,0:T(8,128)} %copy.162) | copy-start | bytes 589828
  209.3 2.3 copy-start.27
  209.3 2.3 copy-start.28
  211.6 3.0 %copy-start.23 = (bf16[256,192]{1,0:T(8,128)(2,1)S(1)}, bf16[256,192]{1,0:T(8,128)(2,1)}, u32[]{:S(2)}) copy-start(bf16[256,192]{1,0:T(8,128)(2,1)} %slice.193) | copy-start | bytes 294916
  211.6 3.0 %copy-start.29 = (f32[256]{0:T(256)S(1)}, f32[256]{0:T(256)}, u32[]{:S(2)}) copy-start(f32[256]{0:T(256)} %get-tuple-element.107) | copy-start | bytes 3076
  213.9 1.3 copy-start.7
  251.4 5.0 %copy-start.20 = (bf16[4,64,768]{2,1,0:T(8,128)(2,1)S(1)}, bf16[4,64,768]{2,1,0:T(8,128)(2,1)}, u32[]{:S(2)}) copy-start(bf16[4,64,768]{2,1,0:T(8,128)(2,1)} %get-tuple-element.34) | copy-start | bytes 1179652

commit v4 on v3

--- a/solution.py
+++ b/solution.py
@@ -248,37 +248,6 @@
         kernel, out_shape=job.outs[0], in_specs=[VM], out_specs=VM, scratch_shapes=job.scratch,
         compiler_params=pltpu.CompilerParams(collective_id=cid, has_side_effects=True),
     )(array)
-
-
-def scatter_sum(blocks, axis, n, cid):
-    shape = blocks.shape[1:]
-
-    def kernel(in_ref, out_ref, land, send, recv):
-        greet((axis, n))
-        me = lax.axis_index(axis)
-        copies = [
-            push(in_ref.at[lax.rem(me + step, n)], land.at[step - 1], send.at[step],
-                 recv.at[step], axis, lax.rem(me + step, n))
-            for step in range(1, n)
-        ]
-        total = in_ref[me].astype(F32)
-        for step, copy in enumerate(copies):
-            copy.wait()
-            total = total + land[step].astype(F32)
-        out_ref[...] = total
-
-    return pl.pallas_call(
-        kernel,
-        out_shape=jax.ShapeDtypeStruct(shape, F32),
-        in_specs=[VM],
-        out_specs=VM,
-        scratch_shapes=[
-            pltpu.VMEM((n - 1,) + shape, blocks.dtype),
-            pltpu.SemaphoreType.DMA((n,)),
-            pltpu.SemaphoreType.DMA((n,)),
-        ],
-        compiler_params=pltpu.CompilerParams(collective_id=cid, has_side_effects=True),
-    )(blocks)
 
 
 def sum_rows_then_gather(partials, extras, middle, gathered, owned, sizes, jobs, cid):
@@ -439,6 +408,62 @@
     )(*args)
 
 
+def attention_backward(q, dcontext, context, kv_all, st_all, q_start, lse, sizes, S, cid):
+    _, n_seq, _ = sizes
+    T, w = q.shape
+    R, h = T // S, w // HD
+    L = R * n_seq
+    scale = 1.0 / math.sqrt(HD)
+
+    def kernel(q_ref, dc_ref, ctx_ref, kv_ref, st_ref, qs_ref, lse_ref, dq_out, dkv_out,
+               block, land, send, recv):
+        greet(("seq", n_seq))
+        seq = lax.axis_index("seq")
+        for s in range(S):
+            rows = slice(s * R, (s + 1) * R)
+            k_start = jnp.concatenate([st_ref[j, s : s + 1, :] for j in range(n_seq)], axis=1)
+            same = qs_ref[rows, :] == k_start
+            dqs, dks, dvs = [], [], []
+            for i in range(h):
+                cols = slice(i * HD, (i + 1) * HD)
+                keys = kv_ref[:, rows, cols].reshape(L, HD)
+                values = kv_ref[:, rows, w + i * HD : w + (i + 1) * HD].reshape(L, HD)
+                query, dc = q_ref[rows, cols], dc_ref[rows, cols]
+                delta = jnp.sum(
+                    dc.astype(F32) * ctx_ref[rows, cols].astype(F32), axis=-1, keepdims=True)
+                scores = jnp.where(same, dot_t(query, keys) * scale, -jnp.inf)
+                probs = jnp.exp(scores - lse_ref[s * h + i])
+                dscores = (probs * (dot_t(dc, values) - delta) * scale).astype(BF)
+                dqs.append(dot(dscores, keys))
+                dks.append(t_dot(dscores, query).astype(BF))
+                dvs.append(t_dot(probs.astype(BF), dc).astype(BF))
+            dq_out[rows, :] = jnp.concatenate(dqs, axis=1)
+            block[:, rows, :] = jnp.concatenate(dks + dvs, axis=1).reshape(n_seq, R, 2 * w)
+        copies = [
+            push(block.at[lax.rem(seq + step, n_seq)], land.at[step - 1], send.at[step],
+                 recv.at[step], "seq", lax.rem(seq + step, n_seq))
+            for step in range(1, n_seq)
+        ]
+        total = block[seq].astype(F32)
+        for step, copy in enumerate(copies):
+            copy.wait()
+            total = total + land[step].astype(F32)
+        dkv_out[...] = total
+
+    sem = pltpu.SemaphoreType.DMA
+    args = (q, dcontext, context, kv_all, st_all, q_start, lse)
+    return pl.pallas_call(
+        kernel,
+        out_shape=[jax.ShapeDtypeStruct((T, w), F32), jax.ShapeDtypeStruct((T, 2 * w), F32)],
+        in_specs=[VM] * len(args), out_specs=[VM] * 2,
+        scratch_shapes=[
+            pltpu.VMEM((n_seq, T, 2 * w), BF), pltpu.VMEM((n_seq - 1, T, 2 * w), BF),
+            sem((n_seq,)), sem((n_seq,)),
+        ],
+        compiler_params=pltpu.CompilerParams(collective_id=cid, has_side_effects=True),
+    )(*args)
+
+
 def make_per_device(mesh):
     n_dp, n_seq, n_ten = mesh.shape["dp"], mesh.shape["seq"], mesh.shape["tensor"]
     sizes = (n_dp, n_seq, n_ten)
@@ -512,29 +537,9 @@
         output = out_rows.astype(F32).reshape(S, R, D)
         dmidb = dmidb.reshape(T, D)
         dcontext = dot(dmidb, w_out_t).astype(BF)
-        k_start = jnp.transpose(starts_all[:, :S], (1, 0, 2)).reshape(S, L)
-        kv_heads = jnp.transpose(
-            kv_all.reshape(n_seq, S, R, 2, h, HD), (3, 1, 4, 0, 2, 5)).reshape(2, S, h, L, HD)
-        keys, values = kv_heads[0], kv_heads[1]
-        qh = jnp.transpose(q.reshape(S, R, h, HD), (0, 2, 1, 3))
-        ctx_h = jnp.transpose(context.reshape(S, R, h, HD), (0, 2, 1, 3))
-        scale = 1.0 / math.sqrt(HD)
-        mask = (starts[:, :, None] == k_start[:, None, :])[:, None]
-        scores = jnp.einsum("shqd,shkd->shqk", qh, keys, preferred_element_type=F32) * scale
-        scores = jnp.where(mask, scores, -jnp.inf)
-        probs32 = jnp.exp(scores - lse.reshape(S, h, R, 1))
-        probs = probs32.astype(BF)
-        dch = jnp.transpose(dcontext.reshape(S, R, h, HD), (0, 2, 1, 3))
-        delta = jnp.sum(dch.astype(F32) * ctx_h.astype(F32), axis=-1, keepdims=True)
-        dprobs = jnp.einsum("shqd,shkd->shqk", dch, values, preferred_element_type=F32)
-        dscores = (probs32 * (dprobs - delta) * scale).astype(BF)
-        dqh = jnp.einsum("shqk,shkd->shqd", dscores, keys, preferred_element_type=F32)
-        dkh = jnp.einsum("shqk,shqd->shkd", dscores, qh, preferred_element_type=F32)
-        dvh = jnp.einsum("shqk,shqd->shkd", probs, dch, preferred_element_type=F32)
-        dkv = jnp.stack([dkh, dvh]).astype(BF).reshape(2, S, h, n_seq, R, HD)
-        dkv = jnp.transpose(dkv, (3, 1, 4, 0, 2, 5)).reshape(n_seq, T, 2 * w)
-        dkv_own = scatter_sum(dkv, "seq", n_seq, 3)
-        dq = unrotate(jnp.transpose(dqh, (0, 2, 1, 3)).reshape(T, h, HD), cosine, sine)
+        dq_rows, dkv_own = attention_backward(
+            q.reshape(T, w), dcontext, context, kv_all, starts_all, q_start, lse, sizes, S, 3)
+        dq = unrotate(dq_rows.reshape(T, h, HD), cosine, sine)
         dk = unrotate(dkv_own[:, :w].reshape(T, h, HD), cosine, sine)
         dqkv = jnp.concatenate(
             [dq.reshape(T, w), dk.reshape(T, w), dkv_own[:, w:]], axis=1).astype(BF)

time: 258 us -> 229 us (0.89)
  local copies, waits for them, and re-layouts: 45.1 us -> 29.1 us
  other arithmetic: 24.3 us -> 15.3 us
  matrix products: 17.4 us -> 11.1 us
  Pallas kernels: 169 us -> 172 us
    reshape x4 -> x0, local copies, waits for them, and re-layouts: 5.94 us -> none  [the longest x2 3.72 us: per_device(): dkv = jnp.transpose(dkv, (3, 1, 4, 0, 2, 5)).reshape(n_seq, T, 2 * w)]
    dot_general x5 -> x0, matrix products: 3.54 us -> none  [the longest x1 1.48 us: per_device(): jnp.einsum('shqd,shkd->shqk', qh, keys, preferred_element_type=F32) * scale]
    pallas_call x1, Pallas kernels: 21.2 us -> 24 us  [attention_backward(): pl.pallas_call(kernel, out_shape=[jax.ShapeDtypeStruct((T, w), F32), jax....]
    transpose x2 -> x0, other arithmetic: 2.64 us -> none  [the longest x1 1.54 us: per_device(): qh = jnp.transpose(q.reshape(S, R, h, HD), (0, 2, 1, 3))]
    convert_element_type x2 -> x1, local copies, waits for them, and re-layouts: 3.39 us -> 0.76 us  [per_device(): dcontext = dot(dmidb, w_out_t).astype(BF)]
where the time goes in v4:
time: 229 us
  Pallas kernels  172 us (75%)
  local copies, waits for them, and re-layouts  29.1 us (13%)
  other arithmetic  15.3 us (7%)
  matrix products  11.1 us (5%)
    pallas_call x2, Pallas kernels, sum_rows_then_gather(): pl.pallas_call(kernel, out_shape=[jax.ShapeDtypeStruct((n,) + s, t) for s...  70.8 us
    pallas_call x1, Pallas kernels, attention_stage(): pl.pallas_call(kernel, out_shape=outs, in_specs=[VM] * len(args), out_spe...  47.9 us
    pallas_call x1, Pallas kernels, gather_weights(): pl.pallas_call(kernel, out_shape=job.outs[0], in_specs=[VM], out_specs=VM...  29.1 us
    pallas_call x1, Pallas kernels, attention_backward(): pl.pallas_call(kernel, out_shape=[jax.ShapeDtypeStruct((T, w), F32), jax....  24 us
    dot_general x4, matrix products, dot(): return jnp.dot(a, b, preferred_element_type=F32)  5.67 us

profile of v4, /device:TPU:0, one launch (start us, length us, event | category | flops | bytes accessed | tf_op | source)
XLA Modules:
  0.0 228.5 jit_solution(15990634954654916317)
XLA Ops:
  0.6 0.8 copy.72
  1.4 0.8 copy.71
  2.2 0.9 copy.69
  3.1 1.1 copy.68
  4.3 0.8 pad_maximum_fusion.9.src
  5.1 29.1 %shard_map.152 = bf16[8,96,770]{2,1,0:T(8,128)(2,1)} custom-call(bf16[96,770]{1,0:T(8,128)(2,1)} %pad_maximum_fusion.9.src), custom_call_target="tpu_custom_call" | custom-call | tf_op jit(solution)/shard_map/pallas_call | solution.py:247
  34.2 1.3 convert_reduce_fusion
  37.3 1.3 copy.73
  38.6 1.6 fusion.28
  40.2 0.8 copy.76
  41.1 0.8 broadcast_subtract_fusion
  42.1 0.7 bitcast_multiply_fusion
  43.0 0.7 maximum_multiply_fusion.1
  43.9 0.8 pad_maximum_fusion.4.kv_ref
  45.5 1.1 copy.78
  46.6 0.7 add_convert_fusion.2.q_ref
  47.3 1.5 copy.80.qs_ref
  48.8 0.9 slice.119.wo_ref
  49.7 0.8 constant_dynamic-slice_fusion
  51.3 0.8 pad_maximum_fusion.10.pb_ref
  52.1 47.9 %shard_map.153 = (bf16[4,64,768]{2,1,0:T(8,128)(2,1)}, f32[64,768]{1,0:T(8,128)}, bf16[256,192]{1,0:T(8,128)(2,1)}, f32[6,128,1]{2,1,0:T(8,128)}, bf16[4,256,384...) custom-call(bf16[256,384]{1,0:T(8,128)(2,1)} %pad_maximum_fusion.4.kv_ref, s32[8,128]{1,0:T(8,128)} %pad.8.st_ref, ...), custom_call_target="tpu_custom_call" | custom-call | tf_op jit(solution)/shard_map/pallas_call | solution.py:401
  100.0 1.9 fusion.2
  102.6 1.3 convolution_convert_fusion.3
  103.9 1.3 convolution_convert_fusion.4
  106.0 1.6 copy.81
  107.6 36.3 %shard_map.154 = (bf16[4,64,768]{2,1,0:T(8,128)(2,1)}, bf16[4,64,768]{2,1,0:T(8,128)(2,1)}, f32[64,768]{1,0:T(8,128)}, f32[1,768]{1,0:T(1,128)}, f32[96,864]{1,0:T(8,128)}) custom-call(bf16[4,64,768]{2,1,0:T(8,128)(2,1)} %bitcast.118, bf16[4,64,768]{2,1,0:T(8,128)(2,1)} %bitcast.99, f32[64,768]{1,0:T(8,128)} %get-tuple-element.27.refs_2_, ...), custom_call_target="tpu_custom_call" | custom-call | tf_op jit(solution)/shard_map/pallas_call | solution.py:302
  143.9 1.9 bitcast_convert_fusion.1
  145.8 1.5 convolution_convert_fusion.6
  147.4 0.8 copy.82.dc_ref
  148.1 24.0 %shard_map.155 = (f32[256,192]{1,0:T(8,128)}, f32[256,384]{1,0:T(8,128)}) custom-call(bf16[256,192]{1,0:T(8,128)(2,1)} %add_convert_fusion.2.q_ref, bf16[256,192]{1,0:T(8,128)(2,1)} %copy.82.dc_ref, bf16[256,192]{1,0:T(8,128)(2,1)} %get-tuple-element.30.ctx_ref, bf16[4,256,384]{2,1,0:T(8,128)(2,1)} %get-tuple-element.31.kv_ref, ...), custom_call_target="tpu_custom_call" | custom-call | tf_op jit(solution)/shard_map/pallas_call | solution.py:455
  172.1 1.7 slice.173
  173.8 1.1 copy.85
  174.9 1.0 slice.100
  176.0 0.7 broadcast_multiply_fusion.1
  177.1 1.0 fusion.27
  178.1 0.8 copy.89
  178.9 1.1 add_convert_fusion.1
  180.0 1.3 multiply_reduce_fusion
  182.9 1.5 copy.90
  185.2 34.5 %shard_map.156 = (bf16[4,64,768]{2,1,0:T(8,128)(2,1)}, f32[96,768]{1,0:T(8,128)}, f32[8,128]{1,0:T(8,128)}) custom-call(bf16[4,64,768]{2,1,0:T(8,128)(2,1)} %bitcast.115, f32[64,768]{1,0:T(8,128)} %get-tuple-element.109.x_ref.refs_1_, f32[64,768]{1,0:T(8,128)} %get-tuple-element.36.refs_2_, f32[1,768]{1,0:T(1,128)} %reshape.229.refs_3_, ...), custom_call_target="tpu_custom_call" | custom-call | tf_op jit(solution)/shard_map/pallas_call | solution.py:302
  219.7 2.0 bitcast_convert_fusion
  221.7 1.0 slice.104
  222.8 0.9 copy.92
  223.7 1.0 slice_bitcast_fusion.2
  224.7 0.7 copy.93
  225.4 0.9 reshape.224
  226.5 0.8 copy.94
  227.3 1.3 slice_bitcast_fusion.3
  (91 shorter events, 8.7 us)
Async XLA Ops:
  4.1 31.3 %copy-start.1 = (f32[2,128,768]{2,1,0:T(8,128)S(1)}, f32[2,128,768]{2,1,0:T(8,128)}, u32[]{:S(2)}) copy-start(f32[2,128,768]{2,1,0:T(8,128)} %param.9) | copy-start | bytes 2359300
  35.5 1.7 copy-start
  41.9 2.9 %copy-start.19 = (s32[2,128]{1,0:T(2,128)}, s32[2,128]{1,0:T(2,128)S(1)}, u32[]{:S(2)}) copy-start(s32[2,128]{1,0:T(2,128)S(1)} %get-tuple-element.101) | copy-start | bytes 3076
  42.1 0.9 copy-start.9
  42.1 1.7 copy-start.11
  43.0 1.0 copy-start.13
  43.0 2.3 %copy-start.8 = (f32[256,192]{0,1:T(8,128)S(1)}, f32[256,192]{0,1:T(8,128)}, u32[]{:S(2)}) copy-start(f32[256,192]{0,1:T(8,128)} %get-tuple-element.91) | copy-start | bytes 589828
  43.9 5.8 %copy-start.5 = (f32[2,128,768]{2,1,0:T(8,128)S(1)}, f32[2,128,768]{2,1,0:T(8,128)}, u32[]{:S(2)}) copy-start(f32[2,128,768]{2,1,0:T(8,128)} %param.17) | copy-start | bytes 2359300
  45.5 5.6 %copy-start.18 = (bf16[288,96]{1,0:T(8,128)(2,1)S(1)}, bf16[288,96]{1,0:T(8,128)(2,1)}, u32[]{:S(2)}) copy-start(bf16[288,96]{1,0:T(8,128)(2,1)} %param.14) | copy-start | bytes 165892
  47.3 3.9 %copy-start.16 = (bf16[96,2,288]{2,1,0:T(2,128)(2,1)S(1)}, bf16[96,2,288]{2,1,0:T(2,128)(2,1)}, u32[]{:S(2)}) copy-start(bf16[96,2,288]{2,1,0:T(2,128)(2,1)} %param.13) | copy-start | bytes 331780
  100.0 1.9 copy-start.2
  103.9 1.6 copy-start.4
  148.1 27.9 %copy-start.12 = (f32[256,64]{0,1:T(8,128)S(1)}, f32[256,64]{0,1:T(8,128)}, u32[]{:S(2)}) copy-start(f32[256,64]{0,1:T(8,128)} %copy-done.11) | copy-start | bytes 196612
  175.9 1.0 copy-start.10
  176.7 2.2 copy-start.6
  176.7 2.2 copy-start.7
  177.1 2.9 %copy-start.21 = (f32[256]{0:T(256)S(1)}, f32[256]{0:T(256)}, u32[]{:S(2)}) copy-start(f32[256]{0:T(256)} %get-tuple-element.97) | copy-start | bytes 3076
  177.1 2.9 %copy-start.22 = (f32[256]{0:T(256)S(1)}, f32[256]{0:T(256)}, u32[]{:S(2)}) copy-start(f32[256]{0:T(256)} %get-tuple-element.99) | copy-start | bytes 3076
  178.9 1.1 copy-start.17
  180.0 1.9 copy-start.3
  180.0 1.9 copy-start.14
  182.9 1.5 copy-start.20
  219.7 5.7 %copy-start.15 = (f32[96,864]{1,0:T(8,128)S(1)}, f32[96,864]{1,0:T(8,128)}, u32[]{:S(2)}) copy-start(f32[96,864]{1,0:T(8,128)} %get-tuple-element.40) | copy-start | bytes 995332
